TPU v7x, 256 devices: a whole 4x4x8 slice. The times are simulated.
256 devices in a mesh: seq: 8 (over z), dp: 32 (over x, y, core).
Axes of the slice: x: 4, y: 4, z: 8, core: 2. Of those that a mesh axis runs over, the one named last changes fastest.
Arguments:
- tokens: bfloat16 [32, 2048, 1408], P('dp', 'seq'), may hold values from -16 to 16
- weights: bfloat16 [1408, 4, 704], P('dp'), may hold values from -2 to 2
- cotangent: bfloat16 [32, 2048, 1408], P('dp', 'seq'), may hold values from -3 to 3
- col_list: int32 [32, 16, 5], P('dp'), may hold values from 0 to 15, as said below
- cut_lengths: int32 [32, 5], P('dp'), may hold values from 1 to 6, 16 in all within a row
- keep_mask: int32 [32, 2048], P('dp'), may hold values 0 or 1
Outputs:
- sublayer_out: bfloat16 [32, 2048, 1408], P('dp', 'seq')
- grad_tokens: bfloat16 [32, 2048, 1408], P('dp', 'seq')
- grad_weights: float32 [1408, 4, 704], P('dp')
Inputs may be any that keep to these rules, and one draw needn't show every extreme that they name: `col_list`: row b lists 5 distinct blocks: b itself first, then blocks within 3 of b, counted cyclically over the packed sequence.
All inputs are finite; a program needn't handle non-finite values. No bound on the sum of `keep_mask` on one device may be relied on, other than what follows from the above.
Results may differ from a plain program's by a relative error of at most 0.038.
Values may be sent and summed in bfloat16 or wider, within the bound.
A program may use at most 128 MiB of HBM per device.

v0:
```python
import math

import jax
import jax.numpy as jnp
from jax import lax
from jax.sharding import PartitionSpec as P

HD = 88


def block_owner(lengths, count):
    ends = jnp.cumsum(lengths, dtype=jnp.int32)
    index = jnp.arange(count, dtype=jnp.int32)
    return jnp.sum((ends[None, :] <= index[:, None]).astype(jnp.int32), axis=1, dtype=jnp.int32)


def allowed_pairs(columns, owner, keep_blocks):
    count, listed = columns.shape
    width = keep_blocks.shape[1]
    same = owner[columns] == owner[:, None]
    kept = keep_blocks[columns] == 1
    itself = columns == jnp.arange(count, dtype=jnp.int32)[:, None]
    diagonal = jnp.eye(width, dtype=bool)
    return same[:, None, :, None] & (
        kept[:, None, :, :] | itself[:, None, :, None] & diagonal[None, :, None, :]
    )


def attend(query_rows, key_rows, value_rows, columns, allowed, heads):
    length = query_rows.shape[0]
    count = columns.shape[0]
    width = length // count
    scale = 1.0 / math.sqrt(HD)
    query_blk = query_rows.reshape(count, width, heads, HD)
    key_blk = key_rows.reshape(count, width, heads, HD)[columns]
    value_blk = value_rows.reshape(count, width, heads, HD)[columns]
    scores = (
        jnp.einsum("bqhd,bnkhd->bhqnk", query_blk, key_blk, preferred_element_type=jnp.float32)
        * scale
    )
    scores = jnp.where(allowed[:, None], scores, -jnp.inf)
    largest = jnp.max(scores, axis=(3, 4), keepdims=True)
    expd = jnp.exp(scores - largest)
    probs = expd / jnp.sum(expd, axis=(3, 4), keepdims=True)
    probs_low = probs.astype(jnp.bfloat16)
    attended = jnp.einsum(
        "bhqnk,bnkhd->bqhd", probs_low, value_blk, preferred_element_type=jnp.float32
    )
    attended = attended.astype(jnp.bfloat16).reshape(length, heads * HD)
    return (attended, probs, probs_low, query_blk, key_blk, value_blk)


def attend_back(d_attended, attended, probs, probs_low, query_blk, key_blk, value_blk, columns):
    count, width, heads, size = query_blk.shape
    scale = 1.0 / math.sqrt(HD)
    d_blk = d_attended.reshape(count, width, heads, size)
    out_blk = attended.reshape(count, width, heads, size)
    delta = jnp.sum(d_blk.astype(jnp.float32) * out_blk.astype(jnp.float32), axis=3)
    delta = jnp.transpose(delta, (0, 2, 1))[:, :, :, None, None]
    d_probs = jnp.einsum("bqhd,bnkhd->bhqnk", d_blk, value_blk, preferred_element_type=jnp.float32)
    d_scores = (probs * (d_probs - delta) * scale).astype(jnp.bfloat16)
    d_query = jnp.einsum("bhqnk,bnkhd->bqhd", d_scores, key_blk, preferred_element_type=jnp.float32)
    d_query = d_query.astype(jnp.bfloat16).reshape(count * width, heads * size)
    d_key_blk = jnp.einsum(
        "bhqnk,bqhd->bnkhd", d_scores, query_blk, preferred_element_type=jnp.float32
    )
    d_value_blk = jnp.einsum(
        "bhqnk,bqhd->bnkhd", probs_low, d_blk, preferred_element_type=jnp.float32
    )
    empty = jnp.zeros((count, width, heads, size), jnp.float32)
    d_key = (
        empty.at[columns].add(d_key_blk).astype(jnp.bfloat16).reshape(count * width, heads * size)
    )
    d_value = (
        empty.at[columns].add(d_value_blk).astype(jnp.bfloat16).reshape(count * width, heads * size)
    )
    return (d_query, d_key, d_value)


def into_heads(stacked):
    return lax.all_to_all(stacked, "seq", split_axis=2, concat_axis=1, tiled=True)


def into_tokens(stacked):
    return lax.all_to_all(stacked, "seq", split_axis=1, concat_axis=2, tiled=True)


def body(tokens, weights, cotangent, col_list, cut_lengths, keep_mask):
    replicas = lax.axis_size("dp")
    inputs = tokens[0]
    upstream = cotangent[0]
    full_weights = lax.all_gather(weights, "dp", axis=0, tiled=True)
    inner = full_weights[:, :3, :]
    outer = full_weights[:, 3, :]
    projected = jnp.einsum("td,dch->cth", inputs, inner, preferred_element_type=jnp.float32).astype(
        jnp.bfloat16
    )
    head_proj = into_heads(projected)
    columns = col_list[0]
    count = columns.shape[0]
    owner = block_owner(cut_lengths[0], count)
    allowed = allowed_pairs(columns, owner, keep_mask[0].reshape(count, -1))
    heads_here = head_proj.shape[2] // HD
    attended, probs, probs_low, query_blk, key_blk, value_blk = attend(
        head_proj[0], head_proj[1], head_proj[2], columns, allowed, heads_here
    )
    attended_tok = into_tokens(attended[None])[0]
    result = jnp.einsum(
        "th,dh->td", attended_tok, outer, preferred_element_type=jnp.float32
    ).astype(jnp.bfloat16)
    d_attended_tok = jnp.dot(upstream, outer, preferred_element_type=jnp.float32).astype(
        jnp.bfloat16
    )
    d_attended = into_heads(d_attended_tok[None])[0]
    d_query, d_key, d_value = attend_back(
        d_attended, attended, probs, probs_low, query_blk, key_blk, value_blk, columns
    )
    d_heads = jnp.stack([d_query, d_key, d_value], axis=0)
    d_proj = into_tokens(d_heads)
    grad_in = jnp.einsum("cth,dch->td", d_proj, inner, preferred_element_type=jnp.float32).astype(
        jnp.bfloat16
    )
    input_rows = lax.all_gather(inputs, "seq", axis=0, tiled=True)
    upstream_rows = lax.all_gather(upstream, "seq", axis=0, tiled=True)
    inner_part = jnp.einsum("td,cth->dch", input_rows, d_heads, preferred_element_type=jnp.float32)
    outer_part = jnp.einsum(
        "td,th->dh", upstream_rows, attended, preferred_element_type=jnp.float32
    )
    local_sum = jnp.concatenate([inner_part, outer_part[:, None, :]], axis=1)
    group_sum = lax.psum_scatter(
        local_sum.astype(jnp.bfloat16), "dp", scatter_dimension=0, tiled=True
    ).astype(jnp.float32)
    total = lax.all_gather(group_sum.astype(jnp.bfloat16), "seq", axis=2, tiled=True).astype(
        group_sum.dtype
    )
    grad_all = total / replicas
    return (result[None], grad_in[None], grad_all)


def solution(mesh):
    placed = (
        P("dp", "seq", None),
        P("dp", None, None),
        P("dp", "seq", None),
        P("dp", None, None),
        P("dp", None),
        P("dp", None),
    )
    return jax.shard_map(
        body,
        mesh=mesh,
        in_specs=placed,
        out_specs=(P("dp", "seq", None), P("dp", "seq", None), P("dp", None, None)),
        check_vma=False,
    )
```

profile of v0, /device:TPU:6, one launch (start us, length us, event | category | flops | bytes accessed | tf_op | source)
XLA Modules:
  0.0 445.9 jit_solution(9382167731238503909)
XLA Ops:
  9.4 62.7 %all-gather.6.cloned.1.call-done = bf16[1408,4,704]{2,1,0:T(4,128)(2,1)} async-done(((bf16[44,4,704]{2,1,0:T(4,128)(2,1)}), bf16[1408,4,704]{2,1,0:T(4,128)(2,1)}) %all-gather.6.cloned.1.call-update) | async-done | bytes 7929872 | tf_op jit(solution)/shard_map/all_gather | solution.py:92
  72.1 7.6 %slice.35 = bf16[1408,1,704]{2,1,0:T(2,128)(2,1)} slice(bf16[1408,4,704]{2,1,0:T(4,128)(2,1)} %all-gather.6.cloned.1.call-done), slice={[0:1408], [3:4], [0:704]} | slice | bytes 3964928 | tf_op jit(solution)/shard_map/slice | solution.py:94
  79.7 12.1 %copy.197 = bf16[1408,1,704]{0,2,1:T(8,128)(2,1)S(1)} copy(bf16[1408,1,704]{2,1,0:T(2,128)(2,1)} %slice.35) | data formatting | bytes 3964928
  93.7 2.9 reduce.5
  97.4 7.0 %all-to-all-start.2 = ((bf16[8,2,11264]{2,1,0:T(2,128)(2,1)}), bf16[8,2,11264]{2,1,0:T(2,128)(2,1)S(1)}, u32[]{:S(2)}, u32[]{:S(2)}) async-start(bf16[8,2,11264]{2,1,0:T(2,128)(2,1)} %reshape.279), calls=%async_computation.2 | async-start | bytes 720896 | tf_op jit(solution)/shard_map/all_to_all | solution.py:81
  104.4 14.2 %copy.198 = bf16[1408,3,704]{0,2,1:T(8,128)(2,1)} copy(bf16[1408,3,704]{2,1,0:T(4,128)(2,1)} %bitcast.181) | data formatting | bytes 11894784
  118.7 4.6 %fusion.25 = bf16[3,256,704]{1,2,0:T(8,128)(2,1)S(1)} fusion(bf16[1408,3,704]{0,2,1:T(8,128)(2,1)} %copy.198, bf16[1,256,1408]{2,1,0:T(8,128)(2,1)S(1)} %copy-done.15), kind=kOutput, calls=%fused_computation.30 | convolution fusion | flops 1523073024 | bytes 7749632 | tf_op jit(solution)/shard_map/td,dch->cth/dot_general | solution.py:95
  125.3 7.5 %all-to-all-start = ((bf16[3,256,704]{1,0,2:T(4,128)(2,1)}), bf16[3,256,704]{1,0,2:T(4,128)(2,1)S(1)}, u32[]{:S(2)}, u32[]{:S(2)}) async-start(bf16[3,256,704]{1,0,2:T(4,128)(2,1)} %copy.141), calls=%async_computation | async-start | bytes 2883584 | tf_op jit(solution)/shard_map/all_to_all | solution.py:81
  137.8 45.8 %all-to-all-done = bf16[3,256,704]{1,0,2:T(4,128)(2,1)S(1)} async-done(((bf16[3,256,704]{1,0,2:T(4,128)(2,1)}), bf16[3,256,704]{1,0,2:T(4,128)(2,1)S(1)}, u32[]{:S(2)}, u32[]{:S(2)}) %all-to-all-start) | async-done | bytes 1081376 | tf_op jit(solution)/shard_map/all_to_all | solution.py:81
  197.7 13.1 %reduce.6 = bf16[2048,88]{1,0:T(8,128)(2,1)S(1)} reduce(bf16[2048,1,88]{2,1,0:T(2,128)(2,1)} %bitcast.190, bf16[]{:T(256)} %broadcast.77), dimensions={1}, to_apply=%bitcast.159.reduce_sub_computation | reduce | bytes 720898
  212.6 4.3 all-to-all-start.1
  216.9 5.3 %multiply_convert_fusion = bf16[16,128,5,128]{1,3,2,0:T(8,128)(2,1)S(1)} fusion(f32[16,128]{1,0:T(8,128)S(1)} %get-tuple-element.20, bf16[16,5,128,88]{2,3,1,0:T(8,128)(2,1)} %bitcast.184, f32[16,128]{1,0:T(8,128)S(1)} %fusion.5, f32[16,128,5,128]{1,3,2,0:T(8,128)} %copy-done.2, f32[16,128]{1,0:T(8,128)S(1)} %get-tuple-element.18, ...), kind=kOutput, calls=%fused_computation.10 | convolution fusion | flops 238551040 | bytes 10051584 | tf_op jit(solution)/shard_map/bqhd,bnkhd->bhqnk/dot_general | solution.py:60
  224.6 5.1 %fusion.44 = f32[16,88,5,128]{3,1,2,0:T(8,128)} fusion(bf16[16,128,5,128]{1,3,2,0:T(8,128)(2,1)} %copy-done.6, bf16[16,128,88,1]{1,0,2,3:T(8,128)(2,1)S(1)} %bitcast.201), kind=kOutput, calls=%fused_computation.50 | convolution fusion | flops 230686720 | bytes 6586368 | tf_op jit(solution)/shard_map/bhqnk,bqhd->bnkhd/dot_general | solution.py:64
  229.8 9.5 %scatter_fusion = f32[16,128,88]{1,2,0:T(8,128)S(1)} fusion(f32[16,128,88]{1,2,0:T(8,128)S(1)} %broadcast.57.clone, s32[80]{0:T(128)S(1)} %reshape.194, f32[80,128,88]{1,2,0:T(8,128)} %bitcast.180), kind=kCustom, calls=%fused_computation.4 | custom fusion | flops 901120 | bytes 10813760 | tf_op jit(solution)/shard_map/scatter-add | solution.py:72
  239.7 4.4 fusion.41
  244.1 9.6 %scatter_fusion.1 = f32[16,128,88]{1,2,0:T(8,128)S(1)} fusion(f32[16,128,88]{1,2,0:T(8,128)S(1)} %broadcast.57.clone.1, s32[80]{0:T(128)S(1)} %reshape.194, f32[80,128,88]{1,2,0:T(8,128)} %bitcast.179), kind=kCustom, calls=%fused_computation.5 | custom fusion | flops 901120 | bytes 10813760 | tf_op jit(solution)/shard_map/scatter-add | solution.py:75
  257.4 5.4 %fusion.10 = bf16[1408,3,88]{0,2,1:T(8,128)(2,1)} fusion(bf16[3,2048,88]{1,2,0:T(8,128)(2,1)S(1)} %constant_dynamic-update-slice_fusion, bf16[1,2048,1408]{2,1,0:T(8,128)(2,1)} %all-gather.8.cloned.1.call-done), kind=kOutput, calls=%fused_computation.19 | convolution fusion | flops 1522904064 | bytes 7591936 | tf_op jit(solution)/shard_map/td,cth->dch/dot_general | solution.py:125
  262.8 7.1 %all-to-all-start.3 = ((bf16[3,2048,88]{2,0,1:T(4,128)(2,1)}), bf16[3,2048,88]{2,0,1:T(4,128)(2,1)S(1)}, u32[]{:S(2)}, u32[]{:S(2)}) async-start(bf16[3,2048,88]{2,0,1:T(4,128)(2,1)} %copy.168), calls=%async_computation.3 | async-start | bytes 4194304 | tf_op jit(solution)/shard_map/all_to_all | solution.py:85
  269.9 3.8 fusion.18
  277.3 117.4 %all-reduce.3.cloned.1.call-done = bf16[1408,4,88]{2,1,0:T(4,128)(2,1)} async-done(((bf16[1408,4,88]{2,1,0:T(4,128)(2,1)}), bf16[1408,4,88]{2,1,0:T(4,128)(2,1)}) %all-reduce.3.cloned.1.call-update) | async-done | bytes 991248
  395.7 27.2 %all_gather.15 = bf16[44,4,704]{0,1,2:T(4,128)(2,1)S(1)} all-gather(bf16[44,4,88]{0,1,2:T(4,128)(2,1)S(1)} %copy.172), channel_id=1, replica_groups=mesh['seq'=8,'dp'=32] {'seq'}, dimensions={2}, use_global_device_ids=true | all-gather | bytes 278784 | tf_op jit(solution)/shard_map/all_gather | solution.py:133
  425.1 3.4 reshape.282
  429.2 3.2 fusion.13
  433.6 5.6 %fusion.14 = bf16[1,256,1408]{2,1,0:T(8,128)(2,1)} fusion(bf16[3,256,704]{1,2,0:T(8,128)(2,1)S(1)} %bitcast.189, bf16[1408,3,704]{0,2,1:T(8,128)(2,1)} %copy.198), kind=kOutput, calls=%fused_computation.21 | convolution fusion | flops 1522892800 | bytes 7749632 | tf_op jit(solution)/shard_map/cth,dch->td/dot_general | solution.py:120
  (122 shorter events, 42.0 us)
Async XLA Ops:
  7.2 126.0 %copy-start = (s32[1,2048]{1,0:T(1,128)S(1)}, s32[1,2048]{1,0:T(1,128)}, u32[]{:S(2)}) copy-start(s32[1,2048]{1,0:T(1,128)} %param.11) | copy-start | bytes 24580
  7.2 65.0 %all-gather.6.cloned.1.call-start = ((), (), s32[]{:S(2)}) async-start(), calls=%async_computation.4 | async-start | bytes 8921088 | tf_op jit(solution)/shard_map/all_gather | solution.py:92
  7.9 249.5 %all-gather.8.cloned.1.call-start = ((), (), s32[]{:S(2)}) async-start(), calls=%async_computation.5 | async-start | bytes 6488064 | tf_op jit(solution)/shard_map/all_gather | solution.py:123
  8.7 261.2 %all-gather.10.cloned.1.call-start = ((), (), s32[]{:S(2)}) async-start(), calls=%async_computation.6 | async-start | bytes 6488064 | tf_op jit(solution)/shard_map/all_gather | solution.py:124
  79.7 12.1 %copy-start.16 = (bf16[1,256,1408]{2,1,0:T(8,128)(2,1)S(1)}, bf16[1,256,1408]{2,1,0:T(8,128)(2,1)}, u32[]{:S(2)}) copy-start(bf16[1,256,1408]{2,1,0:T(8,128)(2,1)} %param.8) | copy-start | bytes 2162692
  91.8 4.8 %copy-start.7 = (bf16[1408,1,704]{0,2,1:T(8,128)(2,1)}, bf16[1408,1,704]{0,2,1:T(8,128)(2,1)S(1)}, u32[]{:S(2)}) copy-start(bf16[1408,1,704]{0,2,1:T(8,128)(2,1)S(1)} %copy.197) | copy-start | bytes 5947396
  97.4 27.9 %all-to-all-start.2 = ((bf16[8,2,11264]{2,1,0:T(2,128)(2,1)}), bf16[8,2,11264]{2,1,0:T(2,128)(2,1)S(1)}, u32[]{:S(2)}, u32[]{:S(2)}) async-start(bf16[8,2,11264]{2,1,0:T(2,128)(2,1)} %reshape.279), calls=%async_computation.2 | async-start | bytes 720896 | tf_op jit(solution)/shard_map/all_to_all | solution.py:81
  104.4 14.2 %copy-start.15 = (bf16[1,256,1408]{2,1,0:T(8,128)(2,1)S(1)}, bf16[1,256,1408]{2,1,0:T(8,128)(2,1)}, u32[]{:S(2)}) copy-start(bf16[1,256,1408]{2,1,0:T(8,128)(2,1)} %param.6) | copy-start | bytes 2162692
  123.3 9.6 %copy-start.17 = (s32[1,16,5]{1,0,2:T(1,128)S(1)}, s32[1,16,5]{1,0,2:T(1,128)}, u32[]{:S(2)}) copy-start(s32[1,16,5]{1,0,2:T(1,128)} %param.9) | copy-start | bytes 964
  123.3 10.6 %copy-start.18 = (s32[1,5]{1,0:T(1,128)S(1)}, s32[1,5]{1,0:T(1,128)}, u32[]{:S(2)}) copy-start(s32[1,5]{1,0:T(1,128)} %param.10) | copy-start | bytes 64
  125.3 58.3 %all-to-all-start = ((bf16[3,256,704]{1,0,2:T(4,128)(2,1)}), bf16[3,256,704]{1,0,2:T(4,128)(2,1)S(1)}, u32[]{:S(2)}, u32[]{:S(2)}) async-start(bf16[3,256,704]{1,0,2:T(4,128)(2,1)} %copy.141), calls=%async_computation | async-start | bytes 2883584 | tf_op jit(solution)/shard_map/all_to_all | solution.py:81
  188.1 2.6 copy-start.3
  188.2 2.4 copy-start.12
  190.7 2.3 copy-start.2
  193.0 1.8 copy-start.10
  195.8 16.9 %copy-start.8 = (bf16[16,128,1,88]{1,3,0,2:T(8,128)(2,1)}, bf16[16,128,1,88]{1,3,0,2:T(8,128)(2,1)S(1)}, u32[]{:S(2)}) copy-start(bf16[16,128,1,88]{1,3,0,2:T(8,128)(2,1)S(1)} %get-tuple-element.21) | copy-start | bytes 1081348
  212.6 50.1 %all-to-all-start.1 = ((bf16[8,2,11264]{2,1,0:T(2,128)(2,1)}), bf16[8,2,11264]{2,1,0:T(2,128)(2,1)}, u32[]{:S(2)}, u32[]{:S(2)}) async-start(bf16[8,2,11264]{2,1,0:T(2,128)(2,1)} %reshape.281), calls=%async_computation.1 | async-start | bytes 720896 | tf_op jit(solution)/shard_map/all_to_all | solution.py:85
  216.9 5.3 %copy-start.4 = (bf16[80,128,88]{1,2,0:T(8,128)(2,1)S(1)}, bf16[80,128,88]{1,2,0:T(8,128)(2,1)}, u32[]{:S(2)}) copy-start(bf16[80,128,88]{1,2,0:T(8,128)(2,1)} %copy-done.3) | copy-start | bytes 5406724
  222.2 2.4 copy-start.13
  262.8 169.7 %all-to-all-start.3 = ((bf16[3,2048,88]{2,0,1:T(4,128)(2,1)}), bf16[3,2048,88]{2,0,1:T(4,128)(2,1)S(1)}, u32[]{:S(2)}, u32[]{:S(2)}) async-start(bf16[3,2048,88]{2,0,1:T(4,128)(2,1)} %copy.168), calls=%async_computation.3 | async-start | bytes 4194304 | tf_op jit(solution)/shard_map/all_to_all | solution.py:85
  269.8 124.9 %all-reduce.3.cloned.1.call-start = ((), (), s32[]{:S(2)}) async-start(), calls=%async_computation.7 | async-start | bytes 2883584
  269.9 3.8 copy-start.14
  273.7 2.4 copy-start.19
  433.6 5.6 %copy-start.1 = (s32[1,2048]{1,0:T(1,128)S(1)}, s32[1,2048]{1,0:T(1,128)}, u32[]{:S(2)}) copy-start(s32[1,2048]{1,0:T(1,128)} %param.11) | copy-start | bytes 24580
  (4 other events, 5.2 us)
Sparse Core Ops, SparseCore 0:
  10.6 61.5 all-gather.5
  73.9 101.4 all-gather.7
  177.2 82.0 all-gather.9
  276.2 118.4 all-reduce.2
where the time goes:
time: 454 us; the launch traced here: 446 us
  waiting for transfers between devices  228 us (50%)
  local copies, waits for them, and re-layouts  69.5 us (15%)
  matrix products  42.2 us (9%)
  other arithmetic  37.7 us (8%)
  blocking collectives  27.2 us (6%)
  starting transfers between devices  26 us (6%)
  between operations  15.2 us (3%)
    unnamed x5, waiting for transfers between devices  119 us
    all_gather x1, waiting for transfers between devices, body(): full_weights = lax.all_gather(weights, 'dp', axis=0, tiled=True)  62.7 us
    all_to_all x2, waiting for transfers between devices, into_heads(): lax.all_to_all(stacked, 'seq', split_axis=2, concat_axis=1, tiled=True)  45.8 us
    unnamed x54, local copies, waits for them, and re-layouts  40.5 us
    all_gather x1, blocking collectives, body(): lax.all_gather(group_sum.astype(jnp.bfloat16), 'seq', axis=2, tiled=True)  27.2 us
    unnamed x2, other arithmetic  16 us
    all_to_all x2, starting transfers between devices, into_heads(): lax.all_to_all(stacked, 'seq', split_axis=2, concat_axis=1, tiled=True)  14.5 us
    all_to_all x2, starting transfers between devices, into_tokens(): lax.all_to_all(stacked, 'seq', split_axis=1, concat_axis=2, tiled=True)  11.3 us
  transfers between devices with their start and end apart: 8, of which 3 were waited for; matrix products, arithmetic and copies ran while one was open for 31% of the time, Pallas kernels for 0%

commit v1 on v0

v1 whole, which is shorter than its diff:
```python
import functools
import math

import jax
import jax.numpy as jnp
from jax import lax
from jax.experimental import pallas as pl
from jax.experimental.pallas import tpu as pltpu
from jax.sharding import PartitionSpec as P

HD = 88
HEADS = 8
HH = 704
D = 1408
OWN = 256
WINDOW = 1024
BLK = 128
NBLK = 16
NX = 4
NY = 4
NZ = 8
CHIP = 88
CUT = 48
NEG = -1e30
MESH = pl.DeviceIdType.MESH
F32 = jnp.float32
BF16 = jnp.bfloat16
ANY = pl.BlockSpec(memory_space=pl.ANY)
VMEM = pl.BlockSpec(memory_space=pltpu.VMEM)


def place():
    seq = lax.axis_index("seq")
    dp = lax.axis_index("dp")
    return seq, dp // (2 * NY), (dp // 2) % NY, dp % 2


def device(seq, x, y, core):
    return (seq, (x * NY + y) * 2 + core)


def greet(others):
    barrier = pltpu.get_barrier_semaphore()
    for other in others:
        pl.semaphore_signal(barrier, inc=1, device_id=other, device_id_type=MESH)
    pl.semaphore_wait(barrier, len(others))


def neighbours(seq, x, y, core):
    return [
        device(seq, x, y, 1 - core),
        device(seq, (x + 1) % NX, y, core),
        device(seq, (x + NX - 1) % NX, y, core),
        device(seq, x, (y + 1) % NY, core),
        device(seq, x, (y + NY - 1) % NY, core),
    ]


def remote(src, dst, send, recv, target):
    return pltpu.make_async_remote_copy(
        src_ref=src, dst_ref=dst, send_sem=send, recv_sem=recv, device_id=target, device_id_type=MESH
    )


def gather_kernel(
    wpad, tok, wfull, win, sib, blk, loc, sz, rz, sx, rx, s1, r1, s2, r2, ss, rs
):
    seq, x, y, core = place()
    up = (seq + 1) % NZ
    down = (seq + NZ - 1) % NZ
    greet(neighbours(seq, x, y, core) + [device(up, x, y, core), device(down, x, y, core)])

    def rows(first, count):
        return win.at[pl.ds(first * BLK, count * BLK)]

    own_tok = pltpu.make_async_copy(tok, rows(3, 2), loc.at[0])
    own_tok.start()
    low, high = tok.at[pl.ds(0, BLK)], tok.at[pl.ds(BLK, BLK)]
    edge_up = remote(high, rows(2, 1), sz.at[0], rz.at[0], device(up, x, y, core))
    edge_down = remote(low, rows(5, 1), sz.at[1], rz.at[1], device(down, x, y, core))
    to_up = remote(low, rows(1, 1), sz.at[4], rz.at[4], device(up, x, y, core))
    to_down = remote(high, rows(6, 1), sz.at[5], rz.at[5], device(down, x, y, core))
    edge_up.start()
    edge_down.start()
    to_up.start()
    to_down.start()
    fwd_up = remote(rows(2, 1), rows(0, 1), sz.at[2], rz.at[2], device(up, x, y, core))
    fwd_down = remote(rows(5, 1), rows(7, 1), sz.at[3], rz.at[3], device(down, x, y, core))

    def weights(c):
        a, b = (x, y) if c == 0 else (y, x)

        def slot(half, aa, bb):
            return wfull.at[half, :, aa, bb] if c == 0 else wfull.at[half, :, bb, aa]

        def at(aa, bb):
            return device(seq, aa, bb, c) if c == 0 else device(seq, bb, aa, c)

        other = device(seq, x, y, 1 - c)
        swap = remote(wpad.at[1 - c], sib, sx.at[0], rx.at[0], other)
        swap.start()
        swap.wait_recv()
        blk[...] = wpad[c] + sib[...]
        own = pltpu.make_async_copy(blk, slot(c, a, b), loc.at[1])
        own.start()
        right1, left1 = (a + 1) % 4, (a + 3) % 4
        right2, left2 = (b + 1) % 4, (b + 3) % 4
        opp1, opp2 = (a + 2) % 4, (b + 2) % 4
        part = (pl.ds(0, CUT), pl.ds(CUT, CHIP - CUT))
        sends = [swap]
        order1 = (a, left1, right1, opp1)

        def send(src, dst, ssem, rsem, target):
            copy = remote(src, dst, ssem, rsem, target)
            copy.start()
            sends.append(copy)

        def arrived(dst, ssem, rsem):
            remote(dst, dst, ssem, rsem, other).wait_recv()

        def share(src, index, aa, bb):
            send(src, slot(c, aa, bb), ss.at[index], rs.at[index], other)

        def second(src, k):
            aa = order1[k]
            send(src, slot(c, aa, b), s2.at[k, 0], r2.at[k, 0], at(a, right2))
            send(src, slot(c, aa, b), s2.at[k, 1], r2.at[k, 1], at(a, left2))

        mine = slot(c, a, b)
        send(blk, mine, s1.at[0], r1.at[0], at(right1, b))
        send(blk, mine, s1.at[1], r1.at[1], at(left1, b))
        second(blk, 0)
        share(blk, 0, a, b)
        left_ref, right_ref = slot(c, left1, b), slot(c, right1, b)
        arrived(left_ref, s1.at[0], r1.at[0])
        send(left_ref.at[:, part[0]], left_ref.at[:, part[0]], s1.at[2], r1.at[2], at(right1, b))
        second(left_ref, 1)
        share(left_ref, 1, left1, b)
        arrived(right_ref, s1.at[1], r1.at[1])
        send(right_ref.at[:, part[1]], right_ref.at[:, part[1]], s1.at[3], r1.at[3], at(left1, b))
        second(right_ref, 2)
        share(right_ref, 2, right1, b)
        opp_ref = slot(c, opp1, b)
        arrived(opp_ref.at[:, part[0]], s1.at[2], r1.at[2])
        arrived(opp_ref.at[:, part[1]], s1.at[3], r1.at[3])
        second(opp_ref, 3)
        share(opp_ref, 3, opp1, b)
        for k in range(4):
            if k == 3:
                edge_up.wait_recv()
                fwd_up.start()
                edge_down.wait_recv()
                fwd_down.start()
            aa = order1[k]
            from_left, from_right = slot(c, aa, left2), slot(c, aa, right2)
            arrived(from_left, s2.at[k, 0], r2.at[k, 0])
            send(from_left.at[:, part[0]], from_left.at[:, part[0]], s2.at[k, 2], r2.at[k, 2], at(a, right2))
            share(from_left, 4 + k, aa, left2)
            arrived(from_right, s2.at[k, 1], r2.at[k, 1])
            send(from_right.at[:, part[1]], from_right.at[:, part[1]], s2.at[k, 3], r2.at[k, 3], at(a, left2))
            share(from_right, 8 + k, aa, right2)
        for k in range(4):
            aa = order1[k]
            far = slot(c, aa, opp2)
            arrived(far.at[:, part[0]], s2.at[k, 2], r2.at[k, 2])
            arrived(far.at[:, part[1]], s2.at[k, 3], r2.at[k, 3])
            share(far, 12 + k, aa, opp2)
        others1 = (b, (b + 3) % 4, (b + 1) % 4, (b + 2) % 4)
        others2 = (a, (a + 3) % 4, (a + 1) % 4, (a + 2) % 4)
        for j in range(4):
            for k in range(4):
                dst = slot(1 - c, others2[j], others1[k])
                arrived(dst, ss.at[4 * j + k], rs.at[4 * j + k])
        for copy in sends:
            copy.wait_send()
        own.wait()

    @pl.when(core == 0)
    def _():
        weights(0)

    @pl.when(core == 1)
    def _():
        weights(1)

    own_tok.wait()
    fwd_up.wait()
    fwd_down.wait()
    to_up.wait()
    to_down.wait()
    edge_up.wait_send()
    edge_down.wait_send()


def gather(wpad, tok):
    dma = pltpu.SemaphoreType.DMA
    return pl.pallas_call(
        gather_kernel,
        out_shape=(
            jax.ShapeDtypeStruct((2, 2, NX, NY, CHIP, HH), BF16),
            jax.ShapeDtypeStruct((8 * BLK, D), BF16),
        ),
        in_specs=[VMEM, ANY],
        out_specs=(ANY, ANY),
        scratch_shapes=[
            pltpu.VMEM((2, CHIP, HH), BF16),
            pltpu.VMEM((2, CHIP, HH), BF16),
            dma((2,)),
            dma((6,)),
            dma((6,)),
            dma((1,)),
            dma((1,)),
            dma((4,)),
            dma((4,)),
            dma((4, 4)),
            dma((4, 4)),
            dma((16,)),
            dma((16,)),
        ],
        compiler_params=pltpu.CompilerParams(
            collective_id=0, has_side_effects=True, vmem_limit_bytes=16 << 20
        ),
        name="gather_weights_halo",
    )(wpad, tok)


NT = (((1,), (1,)), ((), ()))
SCALE = 1.0 / math.sqrt(HD)
SCALE2 = SCALE * math.log2(math.e)
ROWS = (0, 24, 48, 64)
COLS = (0, 320)


def dot(lhs, rhs):
    return jnp.dot(lhs, rhs, preferred_element_type=F32)


def dot_t(lhs, rhs):
    return lax.dot_general(lhs, rhs, NT, preferred_element_type=F32)


class Wave:
    def __init__(self, refs, sems, seq, x, y, core):
        self.g, self.sib, self.p1, self.q1, self.p2, self.q2, self.pieces, self.rz, self.zz = refs
        self.sems = sems
        self.seq, self.core = seq, core
        self.a, self.b = (1 - core) * x + core * y, (1 - core) * y + core * x
        a, b = self.a, self.b
        self.order1 = ((a + 2) % 4, (a + 1) % 4, (a + 3) % 4, a)
        self.order2 = ((b + 2) % 4, (b + 1) % 4, (b + 3) % 4, b)
        self.other = device(seq, x, y, 1 - core)
        self.peers = [device((seq + k) % NZ, x, y, core) for k in range(1, NZ)]
        self.sends = []

    def slot(self, aa, bb):
        return (1 - self.core) * (aa * 4 + bb) + self.core * (bb * 4 + aa)

    def at(self, aa, bb):
        return (self.seq, self.slot(aa, bb) * 2 + self.core)

    def send(self, src, dst, kind, index, target):
        copy = remote(src, dst, self.sems[kind][0].at[index], self.sems[kind][1].at[index], target)
        copy.start()
        self.sends.append(copy)

    def arrived(self, dst, kind, index):
        remote(dst, dst, self.sems[kind][0].at[index], self.sems[kind][1].at[index], self.other).wait_recv()

    def share(self):
        for j in range(4):
            for k in range(4):
                aa, bb = self.order2[k], self.order1[j]
                p = self.core * (aa * 4 + bb) + (1 - self.core) * (bb * 4 + aa)
                self.send(self.g.at[1 - self.core, p], self.sib.at[p], "s", 4 * j + k, self.other)

    def add(self, j, k):
        p = self.slot(self.order1[k], self.order2[j])
        self.arrived(self.sib.at[p], "s", 4 * j + k)
        self.g[self.core, p] = (self.g[self.core, p].astype(F32) + self.sib[p].astype(F32)).astype(BF16)

    def first(self, j):
        self.add(j, 0)
        far = self.g.at[self.core, self.slot(self.order1[0], self.order2[j])]
        for i, part in enumerate((pl.ds(0, CUT), pl.ds(CUT, CHIP - CUT))):
            self.send(far.at[part], self.p1.at[j, part], "1", 4 * j + i, self.at(self.order1[1 + i], self.b))
        for k in range(1, 4):
            self.add(j, k)

    def middle(self, j):
        for i, part in enumerate((pl.ds(0, CUT), pl.ds(CUT, CHIP - CUT))):
            near = self.g.at[self.core, self.slot(self.order1[1 + i], self.order2[j])]
            self.arrived(self.p1.at[j, part], "1", 4 * j + i)
            near[part] = (near[part].astype(F32) + self.p1[j, part].astype(F32)).astype(BF16)
            self.send(near, self.q1.at[j, i], "1", 4 * j + 2 + i, self.at(self.order1[1 + i], self.b))

    def last(self, j):
        own = self.g.at[self.core, self.slot(self.a, self.order2[j])]
        self.arrived(self.q1.at[j, 0], "1", 4 * j + 2)
        self.arrived(self.q1.at[j, 1], "1", 4 * j + 3)
        own[...] = (own[...].astype(F32) + self.q1[j, 0].astype(F32) + self.q1[j, 1].astype(F32)).astype(BF16)
        parts = (pl.ds(0, CUT), pl.ds(CUT, CHIP - CUT))
        if j == 0:
            for i in range(2):
                self.send(own.at[parts[i]], self.p2.at[parts[i]], "2", i, self.at(self.a, self.order2[1 + i]))
        elif j < 3:
            i = j - 1
            part = parts[i]
            self.arrived(self.p2.at[part], "2", i)
            own[part] = (own[part].astype(F32) + self.p2[part].astype(F32)).astype(BF16)
            self.send(own, self.q2.at[i], "2", 2 + i, self.at(self.a, self.order2[1 + i]))

    def spread(self, total):
        own = self.g.at[self.core, self.slot(self.a, self.b)]
        self.arrived(self.q2.at[0], "2", 2)
        self.arrived(self.q2.at[1], "2", 3)
        total[...] = own[...].astype(F32) + self.q2[0].astype(F32) + self.q2[1].astype(F32)
        for piece in range(8):
            r0, c0 = ROWS[piece // 2], COLS[piece % 2]
            self.pieces[piece] = total[r0 : r0 + 24, c0 : c0 + 384].astype(BF16)
        for k in range(1, NZ):
            target = (self.seq + k) % NZ
            self.send(self.pieces.at[target], self.rz.at[k - 1], "z", k - 1, self.peers[k - 1])

    def finish(self):
        acc = self.pieces[self.seq].astype(F32)
        for k in range(1, NZ):
            self.arrived(self.rz.at[k - 1], "z", k - 1)
            acc = acc + self.rz[k - 1].astype(F32)
        self.zz[self.core, self.seq] = acc.astype(BF16)
        mine = self.zz.at[self.core, self.seq]
        for k in range(1, NZ):
            self.send(mine, mine, "g", k - 1, self.peers[k - 1])
        self.send(mine, mine, "w", 0, self.other)

    def pass_on(self):
        for k in range(1, NZ):
            piece = self.zz.at[self.core, (self.seq + NZ - k) % NZ]
            self.arrived(piece, "g", k - 1)
            self.send(piece, piece, "w", k, self.other)

    def collect(self, gout, first, second):
        for k in range(NZ):
            self.arrived(self.zz.at[1 - self.core, (self.seq + NZ - k) % NZ], "w", k)
        for m, index in enumerate((first, second)):
            for piece in range(8):
                r0, c0 = ROWS[piece // 2], COLS[piece % 2]
                gout[index, r0 : r0 + 24, c0 : c0 + 384] = self.zz[m, piece].astype(F32) * (1.0 / 32.0)
        for copy in self.sends:
            copy.wait_send()


def sublayer_kernel(
    tokwin, cot, w, ask, give, give_col, out, gin, gout,
    wv, tw, ct, qh, kh, vh, dh, oh, gh, kg, vg, dwin, bias, stat, sw, rows, tok_t, cot_t, att, dq, dk, dv, total,
    *rest,
):
    refs = [rest[:9], rest[9:18]]
    ld, sd, rd, st, rt = rest[18:23]
    sems = []
    for wave in range(2):
        flat = rest[23 + 12 * wave : 35 + 12 * wave]
        sems.append({kind: (flat[2 * i], flat[2 * i + 1]) for i, kind in enumerate("s12zgw")})
    seq, x, y, core = place()
    up, down = device((seq + 1) % NZ, x, y, core), device((seq + NZ - 1) % NZ, x, y, core)
    up2, down2 = device((seq + 2) % NZ, x, y, core), device((seq + NZ - 2) % NZ, x, y, core)

    loads = [
        pltpu.make_async_copy(cot, ct, ld.at[0]),
        pltpu.make_async_copy(w.at[3], wv.at[3], ld.at[1]),
        pltpu.make_async_copy(tokwin, tw, ld.at[2]),
        pltpu.make_async_copy(w.at[0], wv.at[0], ld.at[3]),
        pltpu.make_async_copy(w.at[1], wv.at[1], ld.at[4]),
        pltpu.make_async_copy(w.at[2], wv.at[2], ld.at[5]),
    ]
    for load in loads:
        load.start()
    greet(neighbours(seq, x, y, core) + [device((seq + k) % NZ, x, y, core) for k in range(1, NZ)])

    loads[0].wait()
    loads[1].wait()
    dwin[3 * BLK : 5 * BLK, :] = dot(ct[...], wv[3]).astype(BF16)

    def around(first, count):
        return dwin.at[pl.ds(first * BLK, count * BLK)]

    halo = [
        remote(around(4, 1), around(2, 1), sd.at[0], rd.at[0], up),
        remote(around(3, 1), around(5, 1), sd.at[1], rd.at[1], down),
        remote(around(3, 1), around(1, 1), sd.at[2], rd.at[2], up),
        remote(around(4, 1), around(6, 1), sd.at[3], rd.at[3], down),
    ]
    for copy in halo:
        copy.start()
    farther = [
        remote(around(2, 1), around(0, 1), sd.at[4], rd.at[4], up),
        remote(around(5, 1), around(7, 1), sd.at[5], rd.at[5], down),
    ]

    for ref in (qh, kh, vh, dh):
        ref[...] = jnp.zeros_like(ref)
    for load in loads[2:]:
        load.wait()

    def project(step, carry):
        at = pl.ds(pl.multiple_of(step * OWN, OWN), OWN)
        rows_in = tw[at, :]
        for m, ref in enumerate((qh, kh, vh)):
            full = dot(rows_in, wv[m]).astype(BF16)
            for h in range(HEADS):
                ref[h, at, 0:HD] = full[:, h * HD : (h + 1) * HD]
        return carry

    lax.fori_loop(0, 4, project, 0)
    for h in range(HEADS):
        dh[h, 3 * BLK : 5 * BLK, 0:HD] = dwin[3 * BLK : 5 * BLK, h * HD : (h + 1) * HD]
    halo[0].wait_recv()
    farther[0].start()
    halo[1].wait_recv()
    farther[1].start()

    row = lax.broadcasted_iota(jnp.int32, (BLK, WINDOW), 0)
    col = lax.broadcasted_iota(jnp.int32, (BLK, WINDOW), 1)
    for i in range(2):
        line = jnp.broadcast_to(ask[i : i + 1, :], (BLK, WINDOW))
        bias[i * BLK : (i + 1) * BLK, :] = jnp.where(col == row + (3 + i) * BLK, 0.0, line)
    lane = lax.broadcasted_iota(jnp.int32, (OWN, BLK), 1)
    stat[...] = jnp.zeros_like(stat)
    mine = slice(3 * BLK, 5 * BLK)

    def ask_head(h, carry):
        k, v, d = kh[h], vh[h], dh[h, mine, :]
        s = dot_t(qh[h, mine, :], k) * SCALE2 + bias[...]
        top = jnp.max(s, axis=1, keepdims=True)
        e = jnp.exp2(s - top)
        norm = jnp.sum(e, axis=1, keepdims=True)
        p = e * (1.0 / norm)
        o = dot(p.astype(BF16), v).astype(BF16)
        oh[h] = o
        delta = jnp.sum(d.astype(F32) * o.astype(F32), axis=1, keepdims=True)
        ds = (p * (dot_t(d, v) - delta)).astype(BF16)
        gh[h] = (dot(ds, k) * SCALE).astype(BF16)
        lse = top + jnp.log2(norm)
        stat[...] = jnp.where(lane == h, lse, jnp.where(lane == h + HEADS, delta, stat[...]))
        return carry

    lax.fori_loop(0, HEADS, ask_head, 0)

    for i in range(2):
        sw[3 + i] = stat[i * BLK : (i + 1) * BLK, :].T[0 : 2 * HEADS, :]
    stats = [
        remote(sw.at[pl.ds(3, 2)], sw.at[pl.ds(1, 2)], st.at[0], rt.at[0], up),
        remote(sw.at[pl.ds(3, 2)], sw.at[pl.ds(5, 2)], st.at[1], rt.at[1], down),
        remote(sw.at[4], sw.at[0], st.at[2], rt.at[2], up2),
        remote(sw.at[3], sw.at[7], st.at[3], rt.at[3], down2),
    ]
    for copy in stats:
        copy.start()

    early = Wave(refs[0], sems[0], seq, x, y, core)
    late = Wave(refs[1], sems[1], seq, x, y, core)

    def partial(dst, lhs, rhs):
        def part(r, carry):
            at = pl.ds(pl.multiple_of(r * 352, 352), 352)
            full = dot(lhs[at, :], rhs[...])
            for k in range(4):
                dst[4 * r + k] = full[k * CHIP : (k + 1) * CHIP, :].astype(BF16)
            return carry

        lax.fori_loop(0, 4, part, 0)

    for h in range(HEADS):
        att[:, h * HD : (h + 1) * HD] = oh[h, :, 0:HD]
        dq[:, h * HD : (h + 1) * HD] = gh[h, :, 0:HD]
    tok_t[...] = tw[mine, :].T
    cot_t[...] = ct[...].T
    partial(early.g.at[0], tok_t, dq)
    partial(early.g.at[1], cot_t, att)
    early.share()

    for i in range(2):
        line = jnp.broadcast_to(give[i : i + 1, :], (BLK, WINDOW)) + give_col[i * BLK : (i + 1) * BLK, :]
        bias[i * BLK : (i + 1) * BLK, :] = jnp.where(col == row + (3 + i) * BLK, 0.0, line)
    early.first(0)
    early.first(1)
    early.first(2)
    early.first(3)
    halo[2].wait_recv()
    halo[3].wait_recv()
    farther[0].wait_recv()
    farther[1].wait_recv()
    for h in range(HEADS):
        dh[h, 0 : 3 * BLK, 0:HD] = dwin[0 : 3 * BLK, h * HD : (h + 1) * HD]
        dh[h, 5 * BLK : 8 * BLK, 0:HD] = dwin[5 * BLK : 8 * BLK, h * HD : (h + 1) * HD]
    for copy in stats:
        copy.wait_recv()
    for i in range(8):
        rows[:, i * BLK : (i + 1) * BLK] = sw[i]

    def give_head(h, carry):
        q, d = qh[h], dh[h]
        lse = rows[pl.ds(h, 1), :]
        delta = rows[pl.ds(h + HEADS, 1), :]
        s = dot_t(kh[h, mine, :], q) * SCALE2 + bias[...]
        p = jnp.exp2(s - lse)
        ds = (p * (dot_t(vh[h, mine, :], d) - delta)).astype(BF16)
        vg[h] = dot(p.astype(BF16), d).astype(BF16)
        kg[h] = (dot(ds, q) * SCALE).astype(BF16)
        return carry

    early.middle(0)
    lax.fori_loop(0, 2, give_head, 0)
    early.middle(1)
    lax.fori_loop(2, 4, give_head, 0)
    early.middle(2)
    early.middle(3)
    early.last(0)
    lax.fori_loop(4, 6, give_head, 0)
    early.last(1)
    lax.fori_loop(6, 8, give_head, 0)
    for h in range(HEADS):
        dk[:, h * HD : (h + 1) * HD] = kg[h, :, 0:HD]
        dv[:, h * HD : (h + 1) * HD] = vg[h, :, 0:HD]
    partial(late.g.at[0], tok_t, dk)
    partial(late.g.at[1], tok_t, dv)
    late.share()
    early.last(2)
    early.last(3)
    for j in range(4):
        late.first(j)
    early.spread(total)
    late.middle(0)
    out[...] = dot_t(att[...], wv[3]).astype(BF16)
    late.middle(1)
    late.middle(2)
    late.middle(3)
    early.finish()
    late.last(0)
    gin[...] = (dot_t(dq[...], wv[0]) + dot_t(dk[...], wv[1]) + dot_t(dv[...], wv[2])).astype(BF16)
    late.last(1)
    late.last(2)
    late.last(3)
    early.pass_on()
    late.spread(total)
    early.collect(gout, 0, 3)
    late.finish()
    late.pass_on()
    late.collect(gout, 1, 2)
    for copy in halo + farther + stats:
        copy.wait_send()


def sublayer(tokwin, cot, w, ask, give, give_col):
    dma = pltpu.SemaphoreType.DMA
    grid16 = (NX * NY, CHIP, HH)
    heads, heads_own = (HEADS, WINDOW, BLK), (HEADS, OWN, BLK)
    bf = lambda *shape: pltpu.VMEM(shape, BF16)
    scratch = [bf(4, D, HH), bf(WINDOW, D), bf(OWN, D)]
    scratch += [bf(*heads)] * 4 + [bf(*heads_own)] * 4
    scratch += [
        bf(WINDOW, HH),
        pltpu.VMEM((OWN, WINDOW), F32),
        pltpu.VMEM((OWN, BLK), F32),
        pltpu.VMEM((8, 2 * HEADS, BLK), F32),
        pltpu.VMEM((2 * HEADS, WINDOW), F32),
        bf(D, OWN),
        bf(D, OWN),
    ]
    scratch += [bf(OWN, HH)] * 4 + [pltpu.VMEM((CHIP, HH), F32)]
    for wave in range(2):
        scratch += [
            bf(2, *grid16),
            bf(*grid16),
            bf(4, CHIP, HH),
            bf(4, 2, CHIP, HH),
            bf(CHIP, HH),
            bf(2, CHIP, HH),
            bf(8, 24, 384),
            bf(7, 24, 384),
            bf(2, 8, 24, 384),
        ]
    scratch += [dma((6,))] + [dma((6,))] * 2 + [dma((4,))] * 2
    for wave in range(2):
        for count in (16, 16, 4, 7, 7, 8):
            scratch += [dma((count,))] * 2
    return pl.pallas_call(
        sublayer_kernel,
        out_shape=(
            jax.ShapeDtypeStruct((OWN, D), BF16),
            jax.ShapeDtypeStruct((OWN, D), BF16),
            jax.ShapeDtypeStruct((4, CHIP, HH), F32),
        ),
        in_specs=[ANY] * 3 + [VMEM] * 3,
        out_specs=(VMEM,) * 3,
        scratch_shapes=scratch,
        compiler_params=pltpu.CompilerParams(
            collective_id=1, has_side_effects=True, vmem_limit_bytes=62 << 20
        ),
        name="sublayer",
    )(tokwin, cot, w, ask, give, give_col)


def biases(columns, lengths, keep):
    seq = lax.axis_index("seq")
    start = (2 * seq + NBLK - 3) % NBLK
    blocks = (start + jnp.arange(8, dtype=jnp.int32)) % NBLK
    mine = 2 * seq + jnp.arange(2, dtype=jnp.int32)
    cut = jnp.arange(lengths.shape[0], dtype=jnp.int32)
    ends = jnp.sum(jnp.where(cut[None, :] <= cut[:, None], lengths[None, :], 0), axis=1)

    def owner(index):
        return jnp.sum((ends[None, :] <= index[:, None]).astype(jnp.int32), axis=1)

    same = owner(mine)[:, None] == owner(blocks)[None, :]
    twice = jnp.concatenate([columns, columns], axis=0)
    columns_mine = lax.dynamic_slice(columns, (2 * seq, 0), (2, columns.shape[1]))
    columns_win = lax.dynamic_slice(twice, (start, 0), (8, columns.shape[1]))
    ask = same & jnp.any(columns_mine[:, None, :] == blocks[None, :, None], axis=2)
    give = same & jnp.any(columns_win[None, :, :] == mine[:, None, None], axis=2)
    kept = keep.reshape(NBLK, BLK)
    kept_win = lax.dynamic_slice(jnp.concatenate([kept, kept], axis=0), (start, 0), (8, BLK))
    kept_mine = lax.dynamic_slice(kept, (2 * seq, 0), (2, BLK))
    ask_rows = jnp.where(ask[:, :, None] & (kept_win == 1)[None], 0.0, NEG).reshape(2, 8 * BLK)
    give_rows = jnp.broadcast_to(jnp.where(give, 0.0, NEG)[:, :, None], (2, 8, BLK)).reshape(2, 8 * BLK)
    give_cols = jnp.where(kept_mine == 1, 0.0, NEG).reshape(2 * BLK, 1)
    return ask_rows.astype(F32), give_rows.astype(F32), give_cols.astype(F32)


def body(tokens, weights, cotangent, col_list, cut_lengths, keep_mask):
    core = lax.axis_index("dp") % 2
    shard = weights.shape[0]
    halves = jnp.transpose(weights, (1, 0, 2)).reshape(2, 2, shard, HH)
    padded = lax.dynamic_update_slice(jnp.zeros((2, 2, CHIP, HH), BF16), halves, (0, 0, shard * core, 0))
    full, window = gather(padded, tokens[0])
    ask, give, give_col = biases(col_list[0], cut_lengths[0], keep_mask[0])
    result, grad_in, summed = sublayer(window, cotangent[0], full.reshape(4, D, HH), ask, give, give_col)
    mine = lax.dynamic_slice(summed, (0, shard * core, 0), (4, shard, HH))
    return (result[None], grad_in[None], jnp.transpose(mine, (1, 0, 2)))


def solution(mesh):
    placed = (
        P("dp", "seq", None),
        P("dp", None, None),
        P("dp", "seq", None),
        P("dp", None, None),
        P("dp", None),
        P("dp", None),
    )
    return jax.shard_map(
        body,
        mesh=mesh,
        in_specs=placed,
        out_specs=(P("dp", "seq", None), P("dp", "seq", None), P("dp", None, None)),
        check_vma=False,
    )
```

time: 454 us -> 142 us (0.31)
  the two profiles are of different devices: /device:TPU:6 before, /device:TPU:1 now
where the time goes in v1:
time: 142 us
  Pallas kernels  120 us (85%)
  local copies, waits for them, and re-layouts  16.7 us (12%)
  other arithmetic  3.81 us (3%)
    pallas_call x1, Pallas kernels, sublayer(): pl.pallas_call(sublayer_kernel, out_shape=(jax.ShapeDtypeStruct((OWN, D),...  81.1 us
    pallas_call x1, Pallas kernels, gather(): pl.pallas_call(gather_kernel, out_shape=(jax.ShapeDtypeStruct((2, 2, NX,...  39.3 us
    unnamed x15, local copies, waits for them, and re-layouts  11.5 us

profile of v1, /device:TPU:1, one launch (start us, length us, event | category | flops | bytes accessed | tf_op | source)
XLA Modules:
  0.0 141.7 jit_solution(2944883809972342076)
XLA Ops:
  0.7 0.8 select_reduce_fusion
  1.5 0.2 convert_reduce_fusion
  1.6 0.2 fusion.5
  1.8 0.7 compare_select_fusion.2
  2.5 0.7 fusion.3
  3.2 0.8 constant_dynamic-slice_fusion.2
  4.0 0.1 copy.19
  4.1 0.2 compare_reduce_fusion.1
  4.4 0.7 copy.30
  5.4 0.2 compare_reduce_fusion
  5.7 0.6 fusion.ask
  6.3 0.6 copy.29
  7.0 0.8 copy.21.give_col
  7.8 1.0 copy.18
  8.8 1.1 dynamic_update_slice.3.wpad
  9.9 1.1 copy-done.2
  11.0 39.3 %gather_weights_halo.1 = (bf16[2,2,4,4,88,704]{5,4,3,2,1,0:T(8,128)(2,1)S(1)}, bf16[1024,1408]{1,0:T(8,128)(2,1)S(1)}) custom-call(bf16[2,2,88,704]{3,2,1,0:T(8,128)(2,1)S(1)} %dynamic_update_slice.3.wpad, bf16[256,1408]{1,0:T(8,128)(2,1)S(1)} %bitcast.30), custom_call_target="tpu_custom_call" | custom-call | tf_op jit(solution)/shard_map/gather_weights_halo/pallas_call | solution.py:197
  50.4 3.3 %copy-done = bf16[2,2,4,4,88,704]{5,4,3,2,1,0:T(8,128)(2,1)} copy-done((bf16[2,2,4,4,88,704]{5,4,3,2,1,0:T(8,128)(2,1)}, bf16[2,2,4,4,88,704]{5,4,3,2,1,0:T(8,128)(2,1)S(1)}, u32[]{:S(2)}) %copy-start) | copy-done | bytes 7929880
  53.6 1.7 %copy-done.1 = bf16[1024,1408]{1,0:T(8,128)(2,1)} copy-done((bf16[1024,1408]{1,0:T(8,128)(2,1)}, bf16[1024,1408]{1,0:T(8,128)(2,1)S(1)}, u32[]{:S(2)}) %copy-start.1) | copy-done | bytes 2883608
  55.3 81.1 %sublayer.1 = (bf16[256,1408]{1,0:T(8,128)(2,1)}, bf16[256,1408]{1,0:T(8,128)(2,1)}, f32[4,88,704]{2,1,0:T(8,128)}) custom-call(bf16[1024,1408]{1,0:T(8,128)(2,1)} %copy-done.1, bf16[256,1408]{1,0:T(8,128)(2,1)} %bitcast.34, bf16[4,1408,704]{2,1,0:T(8,128)(2,1)} %bitcast.29, f32[2,1024]{1,0:T(2,128)} %fusion.ask, f32[2,1024]{1,0:T(2,128)} %bitcast.36, ...), custom_call_target="tpu_custom_call" | custom-call | tf_op jit(solution)/shard_map/sublayer/pallas_call | solution.py:586
  136.5 1.2 dynamic-slice_bitcast_fusion
  137.7 1.1 copy.22
  138.8 2.0 %copy.34 = bf16[1,256,1408]{2,1,0:T(8,128)(2,1)} copy(bf16[1,256,1408]{2,1,0:T(8,128)(2,1)} %bitcast.33) | data formatting | bytes 1441792
  140.8 0.9 copy.35
  (15 shorter events, 0.6 us)
Async XLA Ops:
  9.9 1.1 copy-start.2
  50.3 3.3 %copy-start = (bf16[2,2,4,4,88,704]{5,4,3,2,1,0:T(8,128)(2,1)}, bf16[2,2,4,4,88,704]{5,4,3,2,1,0:T(8,128)(2,1)S(1)}, u32[]{:S(2)}) copy-start(bf16[2,2,4,4,88,704]{5,4,3,2,1,0:T(8,128)(2,1)S(1)} %get-tuple-element.9) | copy-start | bytes 23789572
  53.6 1.7 %copy-start.1 = (bf16[1024,1408]{1,0:T(8,128)(2,1)}, bf16[1024,1408]{1,0:T(8,128)(2,1)S(1)}, u32[]{:S(2)}) copy-start(bf16[1024,1408]{1,0:T(8,128)(2,1)S(1)} %get-tuple-element.8.tokwin) | copy-start | bytes 8650756
  136.4 4.4 %copy-start.3 = (bf16[256,1408]{1,0:T(8,128)(2,1)S(1)}, bf16[256,1408]{1,0:T(8,128)(2,1)}, u32[]{:S(2)}) copy-start(bf16[256,1408]{1,0:T(8,128)(2,1)} %get-tuple-element.11) | copy-start | bytes 2162692

commit v2 on v1

v2 whole, which is shorter than its diff:
```python
import math

import jax
import jax.numpy as jnp
from jax import lax
from jax.experimental import pallas as pl
from jax.experimental.pallas import tpu as pltpu
from jax.sharding import PartitionSpec as P

HD = 88
HEADS = 8
HH = 704
D = 1408
OWN = 256
WINDOW = 1024
BLK = 128
NBLK = 16
NX = 4
NY = 4
NZ = 8
CHIP = 88
CUT = 48
NEG = -1e30
MESH = pl.DeviceIdType.MESH
F32 = jnp.float32
BF16 = jnp.bfloat16
VMEM = pl.BlockSpec(memory_space=pltpu.VMEM)
HBM = pl.BlockSpec(memory_space=pltpu.HBM)
SMEM = pl.BlockSpec(memory_space=pltpu.SMEM)


def place():
    seq = lax.axis_index("seq")
    dp = lax.axis_index("dp")
    return seq, dp // (2 * NY), (dp // 2) % NY, dp % 2


def device(seq, x, y, core):
    return (seq, (x * NY + y) * 2 + core)


def greet(others):
    barrier = pltpu.get_barrier_semaphore()
    for other in others:
        pl.semaphore_signal(barrier, inc=1, device_id=other, device_id_type=MESH)
    pl.semaphore_wait(barrier, len(others))


def neighbours(seq, x, y, core):
    return [
        device(seq, x, y, 1 - core),
        device(seq, (x + 1) % NX, y, core),
        device(seq, (x + NX - 1) % NX, y, core),
        device(seq, x, (y + 1) % NY, core),
        device(seq, x, (y + NY - 1) % NY, core),
    ]


def remote(src, dst, send, recv, target):
    return pltpu.make_async_remote_copy(
        src_ref=src, dst_ref=dst, send_sem=send, recv_sem=recv, device_id=target, device_id_type=MESH
    )


NT = (((1,), (1,)), ((), ()))
SCALE = 1.0 / math.sqrt(HD)
SCALE2 = SCALE * math.log2(math.e)
ROWS = (0, 24, 48, 64)
COLS = (0, 320)


def dot(lhs, rhs):
    return jnp.dot(lhs, rhs, preferred_element_type=F32)


def dot_t(lhs, rhs):
    return lax.dot_general(lhs, rhs, NT, preferred_element_type=F32)


class Gather:
    def __init__(self, wv, blk, sems, seq, x, y, core):
        self.wv, self.blk, self.sems = wv, blk, sems
        self.seq, self.core = seq, core
        self.a, self.b = (1 - core) * x + core * y, (1 - core) * y + core * x
        a, b = self.a, self.b
        self.order1 = (a, (a + 3) % 4, (a + 1) % 4, (a + 2) % 4)
        self.order2 = (b, (b + 3) % 4, (b + 1) % 4, (b + 2) % 4)
        self.other = device(seq, x, y, 1 - core)
        self.sends = []

    def rows(self, half, aa, bb, core, first=0, count=CHIP):
        p = (1 - core) * (aa * 4 + bb) + core * (bb * 4 + aa)
        return self.wv.at[pl.ds(2 * half, 2), p, pl.ds(first, count)]

    def at(self, aa, bb):
        core = self.core
        return (self.seq, ((1 - core) * (aa * 4 + bb) + core * (bb * 4 + aa)) * 2 + core)

    def send(self, src, dst, kind, index, target):
        copy = remote(src, dst, self.sems[kind][0].at[index], self.sems[kind][1].at[index], target)
        copy.start()
        self.sends.append(copy)

    def arrived(self, dst, kind, index):
        remote(dst, dst, self.sems[kind][0].at[index], self.sems[kind][1].at[index], self.other).wait_recv()

    def mine(self, k, j, first=0, count=CHIP):
        return self.rows(self.core, self.order1[k], self.order2[j], self.core, first, count)

    def second(self, src, k):
        for i in range(2):
            self.send(src, self.mine(k, 0), "2", 4 * k + i, self.at(self.a, self.order2[2 - i]))

    def share(self, src, k, j):
        self.send(src, self.mine(k, j), "s", 4 * j + k, self.other)

    def start(self):
        for i in range(2):
            self.send(self.blk, self.mine(0, 0), "1", i, self.at(self.order1[2 - i], self.b))
        self.second(self.blk, 0)
        self.share(self.blk, 0, 0)

    def near(self, i):
        block = self.mine(1 + i, 0)
        self.arrived(block, "1", i)
        part = self.mine(1 + i, 0, CUT * i, (CUT, CHIP - CUT)[i])
        self.send(part, part, "1", 2 + i, self.at(self.order1[2 - i], self.b))
        self.second(block, 1 + i)
        self.share(block, 1 + i, 0)

    def opposite(self):
        self.arrived(self.mine(3, 0, 0, CUT), "1", 2)
        self.arrived(self.mine(3, 0, CUT, CHIP - CUT), "1", 3)
        self.second(self.mine(3, 0), 3)
        self.share(self.mine(3, 0), 3, 0)

    def near2(self, k):
        for i in range(2):
            block = self.mine(k, 1 + i)
            self.arrived(block, "2", 4 * k + i)
            part = self.mine(k, 1 + i, CUT * i, (CUT, CHIP - CUT)[i])
            self.send(part, part, "2", 4 * k + 2 + i, self.at(self.a, self.order2[2 - i]))
            self.share(block, k, 1 + i)

    def far2(self, k):
        self.arrived(self.mine(k, 3, 0, CUT), "2", 4 * k + 2)
        self.arrived(self.mine(k, 3, CUT, CHIP - CUT), "2", 4 * k + 3)
        self.share(self.mine(k, 3), k, 3)

    def finish(self):
        core = self.core
        for j in range(4):
            for k in range(4):
                block = self.rows(1 - core, self.order2[k], self.order1[j], 1 - core)
                self.arrived(block, "s", 4 * j + k)


class Wave:
    def __init__(self, refs, sems, seq, x, y, core):
        self.g, self.sib, self.p1, self.q1, self.p2, self.q2, self.pieces, self.rz, self.zz = refs
        self.sems = sems
        self.seq, self.core = seq, core
        self.a, self.b = (1 - core) * x + core * y, (1 - core) * y + core * x
        a, b = self.a, self.b
        self.order1 = ((a + 2) % 4, (a + 1) % 4, (a + 3) % 4, a)
        self.order2 = ((b + 2) % 4, (b + 1) % 4, (b + 3) % 4, b)
        self.other = device(seq, x, y, 1 - core)
        self.peers = [device((seq + k) % NZ, x, y, core) for k in range(1, NZ)]
        self.sends = []

    def slot(self, aa, bb):
        return (1 - self.core) * (aa * 4 + bb) + self.core * (bb * 4 + aa)

    def at(self, aa, bb):
        return (self.seq, self.slot(aa, bb) * 2 + self.core)

    def send(self, src, dst, kind, index, target):
        copy = remote(src, dst, self.sems[kind][0].at[index], self.sems[kind][1].at[index], target)
        copy.start()
        self.sends.append(copy)

    def arrived(self, dst, kind, index):
        remote(dst, dst, self.sems[kind][0].at[index], self.sems[kind][1].at[index], self.other).wait_recv()

    def share(self):
        for j in range(4):
            for k in range(4):
                aa, bb = self.order2[k], self.order1[j]
                p = self.core * (aa * 4 + bb) + (1 - self.core) * (bb * 4 + aa)
                self.send(self.g.at[1 - self.core, p], self.sib.at[p], "s", 4 * j + k, self.other)

    def add(self, j, k):
        p = self.slot(self.order1[k], self.order2[j])
        self.arrived(self.sib.at[p], "s", 4 * j + k)
        self.g[self.core, p] = (self.g[self.core, p].astype(F32) + self.sib[p].astype(F32)).astype(BF16)

    def first(self, j):
        self.add(j, 0)
        far = self.g.at[self.core, self.slot(self.order1[0], self.order2[j])]
        for i, part in enumerate((pl.ds(0, CUT), pl.ds(CUT, CHIP - CUT))):
            self.send(far.at[part], self.p1.at[j, part], "1", 4 * j + i, self.at(self.order1[1 + i], self.b))
        for k in range(1, 4):
            self.add(j, k)

    def middle(self, j):
        for i, part in enumerate((pl.ds(0, CUT), pl.ds(CUT, CHIP - CUT))):
            near = self.g.at[self.core, self.slot(self.order1[1 + i], self.order2[j])]
            self.arrived(self.p1.at[j, part], "1", 4 * j + i)
            near[part] = (near[part].astype(F32) + self.p1[j, part].astype(F32)).astype(BF16)
            self.send(near, self.q1.at[j, i], "1", 4 * j + 2 + i, self.at(self.order1[1 + i], self.b))

    def last(self, j):
        own = self.g.at[self.core, self.slot(self.a, self.order2[j])]
        self.arrived(self.q1.at[j, 0], "1", 4 * j + 2)
        self.arrived(self.q1.at[j, 1], "1", 4 * j + 3)
        own[...] = (own[...].astype(F32) + self.q1[j, 0].astype(F32) + self.q1[j, 1].astype(F32)).astype(BF16)
        parts = (pl.ds(0, CUT), pl.ds(CUT, CHIP - CUT))
        if j == 0:
            for i in range(2):
                self.send(own.at[parts[i]], self.p2.at[parts[i]], "2", i, self.at(self.a, self.order2[1 + i]))
        elif j < 3:
            i = j - 1
            part = parts[i]
            self.arrived(self.p2.at[part], "2", i)
            own[part] = (own[part].astype(F32) + self.p2[part].astype(F32)).astype(BF16)
            self.send(own, self.q2.at[i], "2", 2 + i, self.at(self.a, self.order2[1 + i]))

    def spread(self, total):
        own = self.g.at[self.core, self.slot(self.a, self.b)]
        self.arrived(self.q2.at[0], "2", 2)
        self.arrived(self.q2.at[1], "2", 3)
        total[...] = own[...].astype(F32) + self.q2[0].astype(F32) + self.q2[1].astype(F32)
        for piece in range(8):
            r0, c0 = ROWS[piece // 2], COLS[piece % 2]
            self.pieces[piece] = total[r0 : r0 + 24, c0 : c0 + 384].astype(BF16)
        for k in range(1, NZ):
            target = (self.seq + k) % NZ
            self.send(self.pieces.at[target], self.rz.at[k - 1], "z", k - 1, self.peers[k - 1])

    def finish(self):
        acc = self.pieces[self.seq].astype(F32)
        for k in range(1, NZ):
            self.arrived(self.rz.at[k - 1], "z", k - 1)
            acc = acc + self.rz[k - 1].astype(F32)
        self.zz[self.core, self.seq] = acc.astype(BF16)
        mine = self.zz.at[self.core, self.seq]
        for k in range(1, NZ):
            self.send(mine, mine, "g", k - 1, self.peers[k - 1])
        self.send(mine, mine, "w", 0, self.other)

    def pass_on(self):
        for k in range(1, NZ):
            piece = self.zz.at[self.core, (self.seq + NZ - k) % NZ]
            self.arrived(piece, "g", k - 1)
            self.send(piece, piece, "w", k, self.other)

    def collect(self, gout, first, second):
        for k in range(NZ):
            self.arrived(self.zz.at[1 - self.core, (self.seq + NZ - k) % NZ], "w", k)
        for m, index in enumerate((first, second)):
            for piece in range(8):
                r0, c0 = ROWS[piece // 2], COLS[piece % 2]
                gout[index, r0 : r0 + 24, c0 : c0 + 384] = self.zz[m, piece].astype(F32) * (1.0 / 32.0)
        for copy in self.sends:
            copy.wait_send()


def sublayer_kernel(
    wsh, tok, cot, cols, cuts, keep, out, gin, gout,
    wv, tw, ct, qh, kh, vh, dh, oh, gh, kg, vg, dwin, bias, bias2, stat, sw, rows, tok_t, cot_t, att, dq, dk, dv,
    total, sib, blk,
    *rest,
):
    refs = [rest[:9], rest[9:18]]
    ld, sd, rd, st, rt = rest[18:23]
    sems = []
    for wave in range(2):
        flat = rest[23 + 12 * wave : 35 + 12 * wave]
        sems.append({kind: (flat[2 * i], flat[2 * i + 1]) for i, kind in enumerate("s12zgw")})
    flat = rest[47:]
    gather_sems = {kind: (flat[2 * i], flat[2 * i + 1]) for i, kind in enumerate("xt12s")}
    seq, x, y, core = place()
    other = device(seq, x, y, 1 - core)
    up, down = device((seq + 1) % NZ, x, y, core), device((seq + NZ - 1) % NZ, x, y, core)
    up2, down2 = device((seq + 2) % NZ, x, y, core), device((seq + NZ - 2) % NZ, x, y, core)

    def halo_rows(first, count):
        return tw.at[pl.ds(first * BLK, count * BLK)]

    load_cot = pltpu.make_async_copy(cot, ct, ld.at[0])
    load_tok = pltpu.make_async_copy(tok, halo_rows(3, 2), ld.at[1])
    load_cot.start()
    load_tok.start()
    greet(neighbours(seq, x, y, core) + [device((seq + k) % NZ, x, y, core) for k in range(1, NZ)])

    swap = remote(
        wsh.at[pl.ds(2 * (1 - core), 2)], sib, gather_sems["x"][0].at[0], gather_sems["x"][1].at[0], other
    )
    swap.start()
    low, high = tok.at[pl.ds(0, BLK)], tok.at[pl.ds(BLK, BLK)]
    tsend, trecv = gather_sems["t"]
    edges = [
        remote(high, halo_rows(2, 1), tsend.at[0], trecv.at[0], up),
        remote(low, halo_rows(5, 1), tsend.at[1], trecv.at[1], down),
        remote(low, halo_rows(1, 1), tsend.at[2], trecv.at[2], up),
        remote(high, halo_rows(6, 1), tsend.at[3], trecv.at[3], down),
    ]
    for copy in edges:
        copy.start()
    edges += [
        remote(halo_rows(2, 1), halo_rows(0, 1), tsend.at[4], trecv.at[4], up),
        remote(halo_rows(5, 1), halo_rows(7, 1), tsend.at[5], trecv.at[5], down),
    ]
    swap.wait_recv()
    ours = wsh[pl.ds(2 * core, 2)]
    theirs = sib[...]
    shard = ours.shape[1]
    blk[:, 0:shard, :] = jnp.where(core == 0, ours, theirs)
    blk[:, shard:CHIP, :] = jnp.where(core == 0, theirs, ours)
    weights = Gather(wv, blk, gather_sems, seq, x, y, core)
    own_rows = pltpu.make_async_copy(blk, weights.mine(0, 0), ld.at[2])
    own_rows.start()
    weights.start()

    blocks = [(2 * seq + NBLK - 3 + i) % NBLK for i in range(8)]
    ends = []
    for c in range(5):
        ends.append(cuts[c] if c == 0 else ends[-1] + cuts[c])

    def owner(index):
        return sum([jnp.where(end <= index, 1, 0) for end in ends])

    owners = [owner(e) for e in blocks]
    row = lax.broadcasted_iota(jnp.int32, (BLK, BLK), 0)
    col = lax.broadcasted_iota(jnp.int32, (BLK, BLK), 1)

    def listed(asks, key):
        found = jnp.where(cols[asks, 0] == key, 1, 0)
        for n in range(1, 5):
            found = found + jnp.where(cols[asks, n] == key, 1, 0)
        return found

    def test(asks, key, same):
        return jnp.where((listed(asks, key) > 0) & same, 0.0, NEG)

    for i in range(2):
        at = slice(i * BLK, (i + 1) * BLK)
        own_keep = jnp.where(keep[pl.ds(blocks[3 + i], 1), :] == 1, 0.0, NEG)
        own_keep = jnp.broadcast_to(own_keep, (BLK, BLK)).T
        for e in range(8):
            same = owners[e] == owners[3 + i]
            line = jnp.where(keep[pl.ds(blocks[e], 1), :] == 1, 0.0, NEG)
            tile = jnp.broadcast_to(line + test(blocks[3 + i], blocks[e], same), (BLK, BLK))
            back = own_keep + test(blocks[e], blocks[3 + i], same)
            if e == 3 + i:
                tile = jnp.where(row == col, 0.0, tile)
                back = jnp.where(row == col, 0.0, back)
            bias[at, e * BLK : (e + 1) * BLK] = tile
            bias2[at, e * BLK : (e + 1) * BLK] = back
    weights.near(0)
    weights.near(1)
    for ref in (qh, kh, vh, dh):
        ref[...] = jnp.zeros_like(ref)
    weights.opposite()
    weights.near2(0)
    weights.near2(1)
    load_cot.wait()
    load_tok.wait()
    weights.near2(2)
    edges[0].wait_recv()
    edges[4].start()
    edges[1].wait_recv()
    edges[5].start()
    weights.near2(3)
    mine = slice(3 * BLK, 5 * BLK)
    tok_t[...] = tw[mine, :].T
    cot_t[...] = ct[...].T
    for k in range(4):
        weights.far2(k)
    weights.finish()
    own_rows.wait()

    dwin[3 * BLK : 5 * BLK, :] = dot(ct[...], wv[3].reshape(D, HH)).astype(BF16)

    def around(first, count):
        return dwin.at[pl.ds(first * BLK, count * BLK)]

    halo = [
        remote(around(4, 1), around(2, 1), sd.at[0], rd.at[0], up),
        remote(around(3, 1), around(5, 1), sd.at[1], rd.at[1], down),
        remote(around(3, 1), around(1, 1), sd.at[2], rd.at[2], up),
        remote(around(4, 1), around(6, 1), sd.at[3], rd.at[3], down),
    ]
    for copy in halo:
        copy.start()
    farther = [
        remote(around(2, 1), around(0, 1), sd.at[4], rd.at[4], up),
        remote(around(5, 1), around(7, 1), sd.at[5], rd.at[5], down),
    ]
    for copy in edges[2:]:
        copy.wait_recv()

    def project(step, carry):
        at = pl.ds(pl.multiple_of(step * OWN, OWN), OWN)
        rows_in = tw[at, :]
        for m, ref in enumerate((qh, kh, vh)):
            full = dot(rows_in, wv[m].reshape(D, HH)).astype(BF16)
            for h in range(HEADS):
                ref[h, at, 0:HD] = full[:, h * HD : (h + 1) * HD]
        return carry

    lax.fori_loop(0, 4, project, 0)
    for h in range(HEADS):
        dh[h, 3 * BLK : 5 * BLK, 0:HD] = dwin[3 * BLK : 5 * BLK, h * HD : (h + 1) * HD]
    halo[0].wait_recv()
    farther[0].start()
    halo[1].wait_recv()
    farther[1].start()

    lane = lax.broadcasted_iota(jnp.int32, (OWN, BLK), 1)
    stat[...] = jnp.zeros_like(stat)

    def ask_head(h, carry):
        k, v, d = kh[h], vh[h], dh[h, mine, :]
        s = dot_t(qh[h, mine, :], k) * SCALE2 + bias[...]
        top = jnp.max(s, axis=1, keepdims=True)
        e = jnp.exp2(s - top)
        norm = jnp.sum(e, axis=1, keepdims=True)
        p = e * (1.0 / norm)
        o = dot(p.astype(BF16), v).astype(BF16)
        oh[h] = o
        delta = jnp.sum(d.astype(F32) * o.astype(F32), axis=1, keepdims=True)
        ds = (p * (dot_t(d, v) - delta)).astype(BF16)
        gh[h] = (dot(ds, k) * SCALE).astype(BF16)
        lse = top + jnp.log2(norm)
        stat[...] = jnp.where(lane == h, lse, jnp.where(lane == h + HEADS, delta, stat[...]))
        return carry

    lax.fori_loop(0, HEADS, ask_head, 0)

    for i in range(2):
        sw[3 + i] = stat[i * BLK : (i + 1) * BLK, :].T[0 : 2 * HEADS, :]
    stats = [
        remote(sw.at[pl.ds(3, 2)], sw.at[pl.ds(1, 2)], st.at[0], rt.at[0], up),
        remote(sw.at[pl.ds(3, 2)], sw.at[pl.ds(5, 2)], st.at[1], rt.at[1], down),
        remote(sw.at[4], sw.at[0], st.at[2], rt.at[2], up2),
        remote(sw.at[3], sw.at[7], st.at[3], rt.at[3], down2),
    ]
    for copy in stats:
        copy.start()

    early = Wave(refs[0], sems[0], seq, x, y, core)
    late = Wave(refs[1], sems[1], seq, x, y, core)

    def partial(dst, lhs, rhs):
        def part(r, carry):
            at = pl.ds(pl.multiple_of(r * 352, 352), 352)
            full = dot(lhs[at, :], rhs[...])
            for k in range(4):
                dst[4 * r + k] = full[k * CHIP : (k + 1) * CHIP, :].astype(BF16)
            return carry

        lax.fori_loop(0, 4, part, 0)

    for h in range(HEADS):
        att[:, h * HD : (h + 1) * HD] = oh[h, :, 0:HD]
        dq[:, h * HD : (h + 1) * HD] = gh[h, :, 0:HD]
    partial(early.g.at[0], tok_t, dq)
    partial(early.g.at[1], cot_t, att)
    early.share()

    early.first(0)
    early.first(1)
    early.first(2)
    early.first(3)
    halo[2].wait_recv()
    halo[3].wait_recv()
    farther[0].wait_recv()
    farther[1].wait_recv()
    for h in range(HEADS):
        dh[h, 0 : 3 * BLK, 0:HD] = dwin[0 : 3 * BLK, h * HD : (h + 1) * HD]
        dh[h, 5 * BLK : 8 * BLK, 0:HD] = dwin[5 * BLK : 8 * BLK, h * HD : (h + 1) * HD]
    for copy in stats:
        copy.wait_recv()
    for i in range(8):
        rows[:, i * BLK : (i + 1) * BLK] = sw[i]

    def give_head(h, carry):
        q, d = qh[h], dh[h]
        lse = rows[pl.ds(h, 1), :]
        delta = rows[pl.ds(h + HEADS, 1), :]
        s = dot_t(kh[h, mine, :], q) * SCALE2 + bias2[...]
        p = jnp.exp2(s - lse)
        ds = (p * (dot_t(vh[h, mine, :], d) - delta)).astype(BF16)
        vg[h] = dot(p.astype(BF16), d).astype(BF16)
        kg[h] = (dot(ds, q) * SCALE).astype(BF16)
        return carry

    early.middle(0)
    lax.fori_loop(0, 2, give_head, 0)
    early.middle(1)
    lax.fori_loop(2, 4, give_head, 0)
    early.middle(2)
    early.middle(3)
    early.last(0)
    lax.fori_loop(4, 6, give_head, 0)
    early.last(1)
    lax.fori_loop(6, 8, give_head, 0)
    for h in range(HEADS):
        dk[:, h * HD : (h + 1) * HD] = kg[h, :, 0:HD]
        dv[:, h * HD : (h + 1) * HD] = vg[h, :, 0:HD]
    partial(late.g.at[0], tok_t, dk)
    partial(late.g.at[1], tok_t, dv)
    late.share()
    early.last(2)
    early.last(3)
    for j in range(4):
        late.first(j)
    early.spread(total)
    late.middle(0)
    out[...] = dot_t(att[...], wv[3].reshape(D, HH)).astype(BF16)
    late.middle(1)
    late.middle(2)
    late.middle(3)
    early.finish()
    late.last(0)
    gin[...] = (dot_t(dq[...], wv[0].reshape(D, HH)) + dot_t(dk[...], wv[1].reshape(D, HH)) + dot_t(dv[...], wv[2].reshape(D, HH))).astype(BF16)
    late.last(1)
    late.last(2)
    late.last(3)
    early.pass_on()
    late.spread(total)
    early.collect(gout, 0, 3)
    late.finish()
    late.pass_on()
    late.collect(gout, 1, 2)
    for copy in halo + farther + stats + edges + weights.sends + [swap]:
        copy.wait_send()


def sublayer(wsh, tok, cot, cols, cuts, keep):
    dma = pltpu.SemaphoreType.DMA
    grid16 = (NX * NY, CHIP, HH)
    heads, heads_own = (HEADS, WINDOW, BLK), (HEADS, OWN, BLK)
    bf = lambda *shape: pltpu.VMEM(shape, BF16)
    scratch = [bf(4, *grid16), bf(WINDOW, D), bf(OWN, D)]
    scratch += [bf(*heads)] * 4 + [bf(*heads_own)] * 4
    scratch += [
        bf(WINDOW, HH),
        pltpu.VMEM((OWN, WINDOW), F32),
        pltpu.VMEM((OWN, WINDOW), F32),
        pltpu.VMEM((OWN, BLK), F32),
        pltpu.VMEM((8, 2 * HEADS, BLK), F32),
        pltpu.VMEM((2 * HEADS, WINDOW), F32),
        bf(D, OWN),
        bf(D, OWN),
    ]
    scratch += [bf(OWN, HH)] * 4 + [pltpu.VMEM((CHIP, HH), F32)]
    scratch += [bf(2, wsh.shape[1], HH), bf(2, CHIP, HH)]
    for wave in range(2):
        scratch += [
            bf(2, *grid16),
            bf(*grid16),
            bf(4, CHIP, HH),
            bf(4, 2, CHIP, HH),
            bf(CHIP, HH),
            bf(2, CHIP, HH),
            bf(8, 24, 384),
            bf(7, 24, 384),
            bf(2, 8, 24, 384),
        ]
    scratch += [dma((3,))] + [dma((6,))] * 2 + [dma((4,))] * 2
    for wave in range(2):
        for count in (16, 16, 4, 7, 7, 8):
            scratch += [dma((count,))] * 2
    for count in (1, 6, 4, 16, 16):
        scratch += [dma((count,))] * 2
    return pl.pallas_call(
        sublayer_kernel,
        out_shape=(
            jax.ShapeDtypeStruct((OWN, D), BF16),
            jax.ShapeDtypeStruct((OWN, D), BF16),
            jax.ShapeDtypeStruct((4, CHIP, HH), F32),
        ),
        in_specs=[VMEM, HBM, HBM, SMEM, SMEM, VMEM],
        out_specs=(VMEM,) * 3,
        scratch_shapes=scratch,
        compiler_params=pltpu.CompilerParams(
            collective_id=1, has_side_effects=True, vmem_limit_bytes=62 << 20
        ),
        name="sublayer",
    )(wsh, tok, cot, cols, cuts, keep)


def body(tokens, weights, cotangent, col_list, cut_lengths, keep_mask):
    core = lax.axis_index("dp") % 2
    shard = weights.shape[0]
    result, grad_in, summed = sublayer(
        jnp.transpose(weights, (1, 0, 2)),
        tokens[0],
        cotangent[0],
        col_list[0],
        cut_lengths[0],
        keep_mask[0].reshape(NBLK, BLK),
    )
    mine = lax.dynamic_slice(summed, (0, shard * core, 0), (4, shard, HH))
    return (result[None], grad_in[None], jnp.transpose(mine, (1, 0, 2)))


def solution(mesh):
    placed = (
        P("dp", "seq", None),
        P("dp", None, None),
        P("dp", "seq", None),
        P("dp", None, None),
        P("dp", None),
        P("dp", None),
    )
    return jax.shard_map(
        body,
        mesh=mesh,
        in_specs=placed,
        out_specs=(P("dp", "seq", None), P("dp", "seq", None), P("dp", None, None)),
        check_vma=False,
    )
```

time: 142 us -> 124 us (0.87)
  local copies, waits for them, and re-layouts: 16.7 us -> 7.12 us
  Pallas kernels: 120 us -> 115 us
  other arithmetic: 3.81 us -> 0 us
    pallas_call x1 -> x0, Pallas kernels: 39.3 us -> none  [gather(): pl.pallas_call(gather_kernel, out_shape=(jax.ShapeDtypeStruct((2, 2, NX,...]
    pallas_call x1, Pallas kernels: 81.1 us -> 115 us  [sublayer(): pl.pallas_call(sublayer_kernel, out_shape=(jax.ShapeDtypeStruct((OWN, D),...]
    unnamed x15 -> x8, local copies, waits for them, and re-layouts: 11.5 us -> 4.57 us
where the time goes in v2:
time: 124 us; the launch traced here: 123 us
  Pallas kernels  115 us (93%)
  local copies, waits for them, and re-layouts  7.12 us (6%)
    pallas_call x1, Pallas kernels, sublayer(): pl.pallas_call(sublayer_kernel, out_shape=(jax.ShapeDtypeStruct((OWN, D),...  115 us
    unnamed x8, local copies, waits for them, and re-layouts  4.57 us

profile of v2, /device:TPU:1, one launch (start us, length us, event | category | flops | bytes accessed | tf_op | source)
XLA Modules:
  0.0 123.3 jit_solution(4563538078099483943)
XLA Ops:
  0.6 1.7 %copy.14 = bf16[44,4,704]{2,0,1:T(8,128)(2,1)} copy(bf16[44,4,704]{2,1,0:T(4,128)(2,1)} %param.7) | data formatting | bytes 495616 | tf_op args[1]
  2.3 1.4 %copy.12 = s32[1,16,5]{2,1,0:T(8,128)} copy(s32[1,16,5]{1,0,2:T(1,128)} %param.9) | data formatting | bytes 640 | tf_op jit(solution)/shard_map/squeeze | solution.py:602
  3.7 115.5 %sublayer.1 = (bf16[256,1408]{1,0:T(8,128)(2,1)}, bf16[256,1408]{1,0:T(8,128)(2,1)}, f32[4,88,704]{2,1,0:T(8,128)}) custom-call(bf16[4,44,704]{2,1,0:T(8,128)(2,1)} %bitcast.12, bf16[256,1408]{1,0:T(8,128)(2,1)} %bitcast.13, bf16[256,1408]{1,0:T(8,128)(2,1)} %bitcast.14, s32[16,5]{1,0:T(8,128)} %bitcast.17, s32[5]{0:T(128)} %bitcast.19, s32[16,128]{1,0:T(8,128)} %bitcast.18), custom_call_target="tpu_custom_call" | custom-call | tf_op jit(solution)/shard_map/sublayer/pallas_call | solution.py:578
  119.2 0.0 copy-start.1
  119.2 1.2 dynamic-slice_bitcast_fusion
  120.4 0.0 copy-start
  120.4 1.1 copy.11
  121.6 0.0 copy-done.1
  121.6 0.9 copy.17
  122.4 0.0 copy-done
  122.4 0.9 copy.18
Async XLA Ops:
  119.2 2.4 %copy-start.1 = (bf16[256,1408]{1,0:T(8,128)(2,1)S(1)}, bf16[256,1408]{1,0:T(8,128)(2,1)}, u32[]{:S(2)}) copy-start(bf16[256,1408]{1,0:T(8,128)(2,1)} %get-tuple-element.6) | copy-start | bytes 2162692
  120.4 2.0 %copy-start = (bf16[256,1408]{1,0:T(8,128)(2,1)S(1)}, bf16[256,1408]{1,0:T(8,128)(2,1)}, u32[]{:S(2)}) copy-start(bf16[256,1408]{1,0:T(8,128)(2,1)} %get-tuple-element.7) | copy-start | bytes 2162692

commit v3 on v2

--- a/solution.py
+++ b/solution.py
@@ -53,6 +53,8 @@
         device(seq, (x + NX - 1) % NX, y, core),
         device(seq, x, (y + 1) % NY, core),
         device(seq, x, (y + NY - 1) % NY, core),
+        device(seq, (x + 2) % NX, y, core),
+        device(seq, x, (y + 2) % NY, core),
     ]
 
 
@@ -88,9 +90,9 @@
         self.other = device(seq, x, y, 1 - core)
         self.sends = []
 
-    def rows(self, half, aa, bb, core, first=0, count=CHIP):
+    def rows(self, half, m, aa, bb, core, first=0, count=CHIP):
         p = (1 - core) * (aa * 4 + bb) + core * (bb * 4 + aa)
-        return self.wv.at[pl.ds(2 * half, 2), p, pl.ds(first, count)]
+        return self.wv.at[2 * half + m, p, pl.ds(first, count)]
 
     def at(self, aa, bb):
         core = self.core
@@ -104,60 +106,62 @@
     def arrived(self, dst, kind, index):
         remote(dst, dst, self.sems[kind][0].at[index], self.sems[kind][1].at[index], self.other).wait_recv()
 
-    def mine(self, k, j, first=0, count=CHIP):
-        return self.rows(self.core, self.order1[k], self.order2[j], self.core, first, count)
-
-    def second(self, src, k):
+    def mine(self, m, k, j, first=0, count=CHIP):
+        return self.rows(self.core, m, self.order1[k], self.order2[j], self.core, first, count)
+
+    def second(self, src, m, k):
         for i in range(2):
-            self.send(src, self.mine(k, 0), "2", 4 * k + i, self.at(self.a, self.order2[2 - i]))
-
-    def share(self, src, k, j):
-        self.send(src, self.mine(k, j), "s", 4 * j + k, self.other)
-
-    def start(self):
+            self.send(src, self.mine(m, k, 0), "2", 16 * m + 4 * k + i, self.at(self.a, self.order2[2 - i]))
+
+    def share(self, src, m, k, j):
+        self.send(src, self.mine(m, k, j), "s", 16 * m + 4 * j + k, self.other)
+
+    def start(self, m):
+        src = self.blk.at[m]
         for i in range(2):
-            self.send(self.blk, self.mine(0, 0), "1", i, self.at(self.order1[2 - i], self.b))
-        self.second(self.blk, 0)
-        self.share(self.blk, 0, 0)
-
-    def near(self, i):
-        block = self.mine(1 + i, 0)
-        self.arrived(block, "1", i)
-        part = self.mine(1 + i, 0, CUT * i, (CUT, CHIP - CUT)[i])
-        self.send(part, part, "1", 2 + i, self.at(self.order1[2 - i], self.b))
-        self.second(block, 1 + i)
-        self.share(block, 1 + i, 0)
-
-    def opposite(self):
-        self.arrived(self.mine(3, 0, 0, CUT), "1", 2)
-        self.arrived(self.mine(3, 0, CUT, CHIP - CUT), "1", 3)
-        self.second(self.mine(3, 0), 3)
-        self.share(self.mine(3, 0), 3, 0)
-
-    def near2(self, k):
+            self.send(src, self.mine(m, 0, 0), "1", 4 * m + i, self.at(self.order1[2 - i], self.b))
+        self.second(src, m, 0)
+        self.share(src, m, 0, 0)
+
+    def near(self, m, i):
+        block = self.mine(m, 1 + i, 0)
+        self.arrived(block, "1", 4 * m + i)
+        part = self.mine(m, 1 + i, 0, CUT * i, (CUT, CHIP - CUT)[i])
+        self.send(part, part, "1", 4 * m + 2 + i, self.at(self.order1[2 - i], self.b))
+        self.second(block, m, 1 + i)
+        self.share(block, m, 1 + i, 0)
+
+    def opposite(self, m):
+        self.arrived(self.mine(m, 3, 0, 0, CUT), "1", 4 * m + 2)
+        self.arrived(self.mine(m, 3, 0, CUT, CHIP - CUT), "1", 4 * m + 3)
+        self.second(self.mine(m, 3, 0), m, 3)
+        self.share(self.mine(m, 3, 0), m, 3, 0)
+
+    def near2(self, m, k):
         for i in range(2):
-            block = self.mine(k, 1 + i)
-            self.arrived(block, "2", 4 * k + i)
-            part = self.mine(k, 1 + i, CUT * i, (CUT, CHIP - CUT)[i])
-            self.send(part, part, "2", 4 * k + 2 + i, self.at(self.a, self.order2[2 - i]))
-            self.share(block, k, 1 + i)
-
-    def far2(self, k):
-        self.arrived(self.mine(k, 3, 0, CUT), "2", 4 * k + 2)
-        self.arrived(self.mine(k, 3, CUT, CHIP - CUT), "2", 4 * k + 3)
-        self.share(self.mine(k, 3), k, 3)
+            block = self.mine(m, k, 1 + i)
+            self.arrived(block, "2", 16 * m + 4 * k + i)
+            part = self.mine(m, k, 1 + i, CUT * i, (CUT, CHIP - CUT)[i])
+            self.send(part, part, "2", 16 * m + 4 * k + 2 + i, self.at(self.a, self.order2[2 - i]))
+            self.share(block, m, k, 1 + i)
+
+    def far2(self, m, k):
+        self.arrived(self.mine(m, k, 3, 0, CUT), "2", 16 * m + 4 * k + 2)
+        self.arrived(self.mine(m, k, 3, CUT, CHIP - CUT), "2", 16 * m + 4 * k + 3)
+        self.share(self.mine(m, k, 3), m, k, 3)
 
     def finish(self):
         core = self.core
-        for j in range(4):
-            for k in range(4):
-                block = self.rows(1 - core, self.order2[k], self.order1[j], 1 - core)
-                self.arrived(block, "s", 4 * j + k)
+        for m in range(2):
+            for j in range(4):
+                for k in range(4):
+                    block = self.rows(1 - core, m, self.order2[k], self.order1[j], 1 - core)
+                    self.arrived(block, "s", 16 * m + 4 * j + k)
 
 
 class Wave:
     def __init__(self, refs, sems, seq, x, y, core):
-        self.g, self.sib, self.p1, self.q1, self.p2, self.q2, self.pieces, self.rz, self.zz = refs
+        self.g, self.sib, self.p1, self.q1, self.q2, self.pieces, self.rz, self.zz = refs
         self.sems = sems
         self.seq, self.core = seq, core
         self.a, self.b = (1 - core) * x + core * y, (1 - core) * y + core * x
@@ -214,22 +218,15 @@
         self.arrived(self.q1.at[j, 0], "1", 4 * j + 2)
         self.arrived(self.q1.at[j, 1], "1", 4 * j + 3)
         own[...] = (own[...].astype(F32) + self.q1[j, 0].astype(F32) + self.q1[j, 1].astype(F32)).astype(BF16)
-        parts = (pl.ds(0, CUT), pl.ds(CUT, CHIP - CUT))
-        if j == 0:
-            for i in range(2):
-                self.send(own.at[parts[i]], self.p2.at[parts[i]], "2", i, self.at(self.a, self.order2[1 + i]))
-        elif j < 3:
-            i = j - 1
-            part = parts[i]
-            self.arrived(self.p2.at[part], "2", i)
-            own[part] = (own[part].astype(F32) + self.p2[part].astype(F32)).astype(BF16)
-            self.send(own, self.q2.at[i], "2", 2 + i, self.at(self.a, self.order2[1 + i]))
+        if j < 3:
+            self.send(own, self.q2.at[j], "2", j, self.at(self.a, self.order2[j]))
 
     def spread(self, total):
-        own = self.g.at[self.core, self.slot(self.a, self.b)]
-        self.arrived(self.q2.at[0], "2", 2)
-        self.arrived(self.q2.at[1], "2", 3)
-        total[...] = own[...].astype(F32) + self.q2[0].astype(F32) + self.q2[1].astype(F32)
+        acc = self.g[self.core, self.slot(self.a, self.b)].astype(F32)
+        for k in range(3):
+            self.arrived(self.q2.at[k], "2", k)
+            acc = acc + self.q2[k].astype(F32)
+        total[...] = acc
         for piece in range(8):
             r0, c0 = ROWS[piece // 2], COLS[piece % 2]
             self.pieces[piece] = total[r0 : r0 + 24, c0 : c0 + 384].astype(BF16)
@@ -271,13 +268,13 @@
     total, sib, blk,
     *rest,
 ):
-    refs = [rest[:9], rest[9:18]]
-    ld, sd, rd, st, rt = rest[18:23]
+    refs = [rest[:8], rest[8:16]]
+    ld, sd, rd, st, rt = rest[16:21]
     sems = []
     for wave in range(2):
-        flat = rest[23 + 12 * wave : 35 + 12 * wave]
+        flat = rest[21 + 12 * wave : 33 + 12 * wave]
         sems.append({kind: (flat[2 * i], flat[2 * i + 1]) for i, kind in enumerate("s12zgw")})
-    flat = rest[47:]
+    flat = rest[45:]
     gather_sems = {kind: (flat[2 * i], flat[2 * i + 1]) for i, kind in enumerate("xt12s")}
     seq, x, y, core = place()
     other = device(seq, x, y, 1 - core)
@@ -293,10 +290,11 @@
     load_tok.start()
     greet(neighbours(seq, x, y, core) + [device((seq + k) % NZ, x, y, core) for k in range(1, NZ)])
 
-    swap = remote(
-        wsh.at[pl.ds(2 * (1 - core), 2)], sib, gather_sems["x"][0].at[0], gather_sems["x"][1].at[0], other
-    )
-    swap.start()
+    swaps = []
+    for m in range(2):
+        xsend, xrecv = gather_sems["x"]
+        swaps.append(remote(wsh.at[2 * (1 - core) + m], sib.at[m], xsend.at[m], xrecv.at[m], other))
+        swaps[m].start()
     low, high = tok.at[pl.ds(0, BLK)], tok.at[pl.ds(BLK, BLK)]
     tsend, trecv = gather_sems["t"]
     edges = [
@@ -311,17 +309,39 @@
         remote(halo_rows(2, 1), halo_rows(0, 1), tsend.at[4], trecv.at[4], up),
         remote(halo_rows(5, 1), halo_rows(7, 1), tsend.at[5], trecv.at[5], down),
     ]
-    swap.wait_recv()
-    ours = wsh[pl.ds(2 * core, 2)]
-    theirs = sib[...]
-    shard = ours.shape[1]
-    blk[:, 0:shard, :] = jnp.where(core == 0, ours, theirs)
-    blk[:, shard:CHIP, :] = jnp.where(core == 0, theirs, ours)
     weights = Gather(wv, blk, gather_sems, seq, x, y, core)
-    own_rows = pltpu.make_async_copy(blk, weights.mine(0, 0), ld.at[2])
-    own_rows.start()
-    weights.start()
-
+    own_rows = []
+    for m in range(2):
+        swaps[m].wait_recv()
+        ours = wsh[2 * core + m]
+        theirs = sib[m]
+        shard = ours.shape[0]
+        blk[m, 0:shard, :] = jnp.where(core == 0, ours, theirs)
+        blk[m, shard:CHIP, :] = jnp.where(core == 0, theirs, ours)
+        own_rows.append(pltpu.make_async_copy(blk.at[m], weights.mine(m, 0, 0), ld.at[2 + m]))
+        own_rows[m].start()
+        weights.start(m)
+
+    for m in range(2):
+        weights.near(m, 0)
+        weights.near(m, 1)
+        weights.near2(m, 0)
+    for m in range(2):
+        weights.opposite(m)
+    weights.near2(0, 1)
+    weights.near2(1, 1)
+    weights.far2(0, 0)
+    weights.near2(0, 2)
+    weights.far2(1, 0)
+    weights.near2(1, 2)
+    edges[0].wait_recv()
+    edges[4].start()
+    edges[1].wait_recv()
+    edges[5].start()
+    weights.near2(0, 3)
+    weights.near2(1, 3)
+    load_cot.wait()
+    load_tok.wait()
     blocks = [(2 * seq + NBLK - 3 + i) % NBLK for i in range(8)]
     ends = []
     for c in range(5):
@@ -335,9 +355,9 @@
     col = lax.broadcasted_iota(jnp.int32, (BLK, BLK), 1)
 
     def listed(asks, key):
-        found = jnp.where(cols[asks, 0] == key, 1, 0)
+        found = jnp.where(cols[0, asks] == key, 1, 0)
         for n in range(1, 5):
-            found = found + jnp.where(cols[asks, n] == key, 1, 0)
+            found = found + jnp.where(cols[n, asks] == key, 1, 0)
         return found
 
     def test(asks, key, same):
@@ -357,28 +377,17 @@
                 back = jnp.where(row == col, 0.0, back)
             bias[at, e * BLK : (e + 1) * BLK] = tile
             bias2[at, e * BLK : (e + 1) * BLK] = back
-    weights.near(0)
-    weights.near(1)
     for ref in (qh, kh, vh, dh):
         ref[...] = jnp.zeros_like(ref)
-    weights.opposite()
-    weights.near2(0)
-    weights.near2(1)
-    load_cot.wait()
-    load_tok.wait()
-    weights.near2(2)
-    edges[0].wait_recv()
-    edges[4].start()
-    edges[1].wait_recv()
-    edges[5].start()
-    weights.near2(3)
     mine = slice(3 * BLK, 5 * BLK)
     tok_t[...] = tw[mine, :].T
     cot_t[...] = ct[...].T
-    for k in range(4):
-        weights.far2(k)
+    for k in range(1, 4):
+        for m in range(2):
+            weights.far2(m, k)
     weights.finish()
-    own_rows.wait()
+    for copy in own_rows:
+        copy.wait()
 
     dwin[3 * BLK : 5 * BLK, :] = dot(ct[...], wv[3].reshape(D, HH)).astype(BF16)
 
@@ -403,13 +412,20 @@
     def project(step, carry):
         at = pl.ds(pl.multiple_of(step * OWN, OWN), OWN)
         rows_in = tw[at, :]
-        for m, ref in enumerate((qh, kh, vh)):
+        for m, ref in ((1, kh), (2, vh)):
             full = dot(rows_in, wv[m].reshape(D, HH)).astype(BF16)
             for h in range(HEADS):
                 ref[h, at, 0:HD] = full[:, h * HD : (h + 1) * HD]
         return carry
 
+    def queries(first, count):
+        at = slice(first * BLK, (first + count) * BLK)
+        full = dot(tw[at, :], wv[0].reshape(D, HH)).astype(BF16)
+        for h in range(HEADS):
+            qh[h, at, 0:HD] = full[:, h * HD : (h + 1) * HD]
+
     lax.fori_loop(0, 4, project, 0)
+    queries(3, 2)
     for h in range(HEADS):
         dh[h, 3 * BLK : 5 * BLK, 0:HD] = dwin[3 * BLK : 5 * BLK, h * HD : (h + 1) * HD]
     halo[0].wait_recv()
@@ -468,11 +484,9 @@
     partial(early.g.at[0], tok_t, dq)
     partial(early.g.at[1], cot_t, att)
     early.share()
-
-    early.first(0)
-    early.first(1)
-    early.first(2)
-    early.first(3)
+    queries(0, 3)
+    queries(5, 3)
+
     halo[2].wait_recv()
     halo[3].wait_recv()
     farther[0].wait_recv()
@@ -480,6 +494,8 @@
     for h in range(HEADS):
         dh[h, 0 : 3 * BLK, 0:HD] = dwin[0 : 3 * BLK, h * HD : (h + 1) * HD]
         dh[h, 5 * BLK : 8 * BLK, 0:HD] = dwin[5 * BLK : 8 * BLK, h * HD : (h + 1) * HD]
+    early.first(0)
+    early.first(1)
     for copy in stats:
         copy.wait_recv()
     for i in range(8):
@@ -496,15 +512,15 @@
         kg[h] = (dot(ds, q) * SCALE).astype(BF16)
         return carry
 
+    lax.fori_loop(0, 2, give_head, 0)
+    early.first(2)
+    early.first(3)
     early.middle(0)
-    lax.fori_loop(0, 2, give_head, 0)
+    lax.fori_loop(2, 4, give_head, 0)
     early.middle(1)
-    lax.fori_loop(2, 4, give_head, 0)
+    lax.fori_loop(4, 6, give_head, 0)
     early.middle(2)
     early.middle(3)
-    early.last(0)
-    lax.fori_loop(4, 6, give_head, 0)
-    early.last(1)
     lax.fori_loop(6, 8, give_head, 0)
     for h in range(HEADS):
         dk[:, h * HD : (h + 1) * HD] = kg[h, :, 0:HD]
@@ -512,29 +528,37 @@
     partial(late.g.at[0], tok_t, dk)
     partial(late.g.at[1], tok_t, dv)
     late.share()
+    early.last(0)
+    out[...] = dot_t(att[...], wv[3].reshape(D, HH)).astype(BF16)
+    early.last(1)
+    late.first(0)
     early.last(2)
+    late.first(1)
+    late.middle(0)
     early.last(3)
-    for j in range(4):
-        late.first(j)
+    late.first(2)
+    late.middle(1)
     early.spread(total)
-    late.middle(0)
-    out[...] = dot_t(att[...], wv[3].reshape(D, HH)).astype(BF16)
-    late.middle(1)
+    late.first(3)
     late.middle(2)
+    late.last(0)
     late.middle(3)
+    late.last(1)
     early.finish()
-    late.last(0)
-    gin[...] = (dot_t(dq[...], wv[0].reshape(D, HH)) + dot_t(dk[...], wv[1].reshape(D, HH)) + dot_t(dv[...], wv[2].reshape(D, HH))).astype(BF16)
-    late.last(1)
     late.last(2)
     late.last(3)
     early.pass_on()
     late.spread(total)
+    gin[...] = (
+        dot_t(dq[...], wv[0].reshape(D, HH))
+        + dot_t(dk[...], wv[1].reshape(D, HH))
+        + dot_t(dv[...], wv[2].reshape(D, HH))
+    ).astype(BF16)
     early.collect(gout, 0, 3)
     late.finish()
     late.pass_on()
     late.collect(gout, 1, 2)
-    for copy in halo + farther + stats + edges + weights.sends + [swap]:
+    for copy in halo + farther + stats + edges + weights.sends + swaps:
         copy.wait_send()
 
 
@@ -563,17 +587,16 @@
             bf(*grid16),
             bf(4, CHIP, HH),
             bf(4, 2, CHIP, HH),
-            bf(CHIP, HH),
-            bf(2, CHIP, HH),
+            bf(3, CHIP, HH),
             bf(8, 24, 384),
             bf(7, 24, 384),
             bf(2, 8, 24, 384),
         ]
-    scratch += [dma((3,))] + [dma((6,))] * 2 + [dma((4,))] * 2
+    scratch += [dma((4,))] + [dma((6,))] * 2 + [dma((4,))] * 2
     for wave in range(2):
-        for count in (16, 16, 4, 7, 7, 8):
+        for count in (16, 16, 3, 7, 7, 8):
             scratch += [dma((count,))] * 2
-    for count in (1, 6, 4, 16, 16):
+    for count in (2, 6, 8, 32, 32):
         scratch += [dma((count,))] * 2
     return pl.pallas_call(
         sublayer_kernel,
@@ -599,7 +622,7 @@
         jnp.transpose(weights, (1, 0, 2)),
         tokens[0],
         cotangent[0],
-        col_list[0],
+        col_list[0].T,
         cut_lengths[0],
         keep_mask[0].reshape(NBLK, BLK),
     )

time: 124 us -> 121 us (0.976)
  Pallas kernels: 115 us -> 113 us
    pallas_call x1, Pallas kernels: 115 us -> 113 us  [sublayer(): pl.pallas_call(sublayer_kernel, out_shape=(jax.ShapeDtypeStruct((OWN, D),...]
    squeeze x1 -> x0, local copies, waits for them, and re-layouts: 1.36 us -> none  [body(): col_list[0]]
    unnamed x8 -> x9, local copies, waits for them, and re-layouts: 4.57 us -> 5.85 us
where the time goes in v3:
time: 121 us; the launch traced here: 120 us
  Pallas kernels  113 us (93%)
  local copies, waits for them, and re-layouts  7.04 us (6%)
    pallas_call x1, Pallas kernels, sublayer(): pl.pallas_call(sublayer_kernel, out_shape=(jax.ShapeDtypeStruct((OWN, D),...  113 us
    unnamed x9, local copies, waits for them, and re-layouts  5.85 us

profile of v3, /device:TPU:1, one launch (start us, length us, event | category | flops | bytes accessed | tf_op | source)
XLA Modules:
  0.0 120.4 jit_solution(1729546780277166798)
XLA Ops:
  0.6 1.7 %copy.14 = bf16[44,4,704]{2,0,1:T(8,128)(2,1)} copy(bf16[44,4,704]{2,1,0:T(4,128)(2,1)} %param.7) | data formatting | bytes 495616 | tf_op args[1]
  2.3 1.3 %copy.15 = s32[1,16,5]{1,2,0:T(8,128)} copy(s32[1,16,5]{1,0,2:T(1,128)} %param.9) | data formatting | bytes 640
  3.6 112.6 %sublayer.1 = (bf16[256,1408]{1,0:T(8,128)(2,1)}, bf16[256,1408]{1,0:T(8,128)(2,1)}, f32[4,88,704]{2,1,0:T(8,128)}) custom-call(bf16[4,44,704]{2,1,0:T(8,128)(2,1)} %bitcast.16, bf16[256,1408]{1,0:T(8,128)(2,1)} %bitcast.17, bf16[256,1408]{1,0:T(8,128)(2,1)} %bitcast.18, s32[5,16]{1,0:T(8,128)} %bitcast.21, s32[5]{0:T(128)} %bitcast.23, s32[16,128]{1,0:T(8,128)} %bitcast.22), custom_call_target="tpu_custom_call" | custom-call | tf_op jit(solution)/shard_map/sublayer/pallas_call | solution.py:601
  116.3 0.0 copy-start.1
  116.3 1.2 dynamic-slice_bitcast_fusion
  117.5 0.0 copy-start
  117.5 1.1 copy.10
  118.6 0.0 copy-done.1
  118.6 0.9 copy.18
  119.5 0.0 copy-done
  119.5 0.9 copy.19
Async XLA Ops:
  116.3 2.4 %copy-start.1 = (bf16[256,1408]{1,0:T(8,128)(2,1)S(1)}, bf16[256,1408]{1,0:T(8,128)(2,1)}, u32[]{:S(2)}) copy-start(bf16[256,1408]{1,0:T(8,128)(2,1)} %get-tuple-element.6) | copy-start | bytes 2162692
  117.5 2.0 %copy-start = (bf16[256,1408]{1,0:T(8,128)(2,1)S(1)}, bf16[256,1408]{1,0:T(8,128)(2,1)}, u32[]{:S(2)}) copy-start(bf16[256,1408]{1,0:T(8,128)(2,1)} %get-tuple-element.7) | copy-start | bytes 2162692

commit v4 on v3

--- a/solution.py
+++ b/solution.py
@@ -69,6 +69,7 @@
 SCALE2 = SCALE * math.log2(math.e)
 ROWS = (0, 24, 48, 64)
 COLS = (0, 320)
+FAR_FIRST = (4, 3, 5, 2, 6, 1, 7)
 
 
 def dot(lhs, rhs):
@@ -230,7 +231,7 @@
         for piece in range(8):
             r0, c0 = ROWS[piece // 2], COLS[piece % 2]
             self.pieces[piece] = total[r0 : r0 + 24, c0 : c0 + 384].astype(BF16)
-        for k in range(1, NZ):
+        for k in FAR_FIRST:
             target = (self.seq + k) % NZ
             self.send(self.pieces.at[target], self.rz.at[k - 1], "z", k - 1, self.peers[k - 1])
 
@@ -241,12 +242,12 @@
             acc = acc + self.rz[k - 1].astype(F32)
         self.zz[self.core, self.seq] = acc.astype(BF16)
         mine = self.zz.at[self.core, self.seq]
-        for k in range(1, NZ):
+        for k in FAR_FIRST:
             self.send(mine, mine, "g", k - 1, self.peers[k - 1])
         self.send(mine, mine, "w", 0, self.other)
 
     def pass_on(self):
-        for k in range(1, NZ):
+        for k in FAR_FIRST[::-1]:
             piece = self.zz.at[self.core, (self.seq + NZ - k) % NZ]
             self.arrived(piece, "g", k - 1)
             self.send(piece, piece, "w", k, self.other)
@@ -554,8 +555,8 @@
         + dot_t(dk[...], wv[1].reshape(D, HH))
         + dot_t(dv[...], wv[2].reshape(D, HH))
     ).astype(BF16)
+    late.finish()
     early.collect(gout, 0, 3)
-    late.finish()
     late.pass_on()
     late.collect(gout, 1, 2)
     for copy in halo + farther + stats + edges + weights.sends + swaps:

time: 121 us -> 118 us (0.975)
  Pallas kernels: 113 us -> 110 us
    pallas_call x1, Pallas kernels: 113 us -> 110 us  [sublayer(): pl.pallas_call(sublayer_kernel, out_shape=(jax.ShapeDtypeStruct((OWN, D),...]
where the time goes in v4:
time: 118 us; the launch traced here: 117 us
  Pallas kernels  110 us (93%)
  local copies, waits for them, and re-layouts  7.04 us (6%)
    pallas_call x1, Pallas kernels, sublayer(): pl.pallas_call(sublayer_kernel, out_shape=(jax.ShapeDtypeStruct((OWN, D),...  110 us
    unnamed x9, local copies, waits for them, and re-layouts  5.85 us

profile of v4, /device:TPU:1, one launch (start us, length us, event | category | flops | bytes accessed | tf_op | source)
XLA Modules:
  0.0 117.4 jit_solution(17362218015982450195)
XLA Ops:
  0.6 1.7 %copy.14 = bf16[44,4,704]{2,0,1:T(8,128)(2,1)} copy(bf16[44,4,704]{2,1,0:T(4,128)(2,1)} %param.7) | data formatting | bytes 495616 | tf_op args[1]
  2.3 1.3 %copy.15 = s32[1,16,5]{1,2,0:T(8,128)} copy(s32[1,16,5]{1,0,2:T(1,128)} %param.9) | data formatting | bytes 640
  3.6 109.7 %sublayer.1 = (bf16[256,1408]{1,0:T(8,128)(2,1)}, bf16[256,1408]{1,0:T(8,128)(2,1)}, f32[4,88,704]{2,1,0:T(8,128)}) custom-call(bf16[4,44,704]{2,1,0:T(8,128)(2,1)} %bitcast.16, bf16[256,1408]{1,0:T(8,128)(2,1)} %bitcast.17, bf16[256,1408]{1,0:T(8,128)(2,1)} %bitcast.18, s32[5,16]{1,0:T(8,128)} %bitcast.21, s32[5]{0:T(128)} %bitcast.23, s32[16,128]{1,0:T(8,128)} %bitcast.22), custom_call_target="tpu_custom_call" | custom-call | tf_op jit(solution)/shard_map/sublayer/pallas_call | solution.py:602
  113.4 0.0 copy-start.1
  113.4 1.2 %dynamic-slice_bitcast_fusion = f32[44,4,704]{2,0,1:T(8,128)S(1)} fusion(f32[4,88,704]{2,1,0:T(8,128)} %get-tuple-element.8, s32[]{:T(128)S(6)} %select_n.11), kind=kLoop, calls=%fused_computation | loop fusion | bytes 991236 | tf_op jit(solution)/shard_map/transpose | solution.py:631
  114.6 0.0 copy-start
  114.6 1.1 copy.10
  115.7 0.0 copy-done.1
  115.7 0.9 copy.18
  116.6 0.0 copy-done
  116.6 0.9 copy.19
Async XLA Ops:
  113.4 2.4 %copy-start.1 = (bf16[256,1408]{1,0:T(8,128)(2,1)S(1)}, bf16[256,1408]{1,0:T(8,128)(2,1)}, u32[]{:S(2)}) copy-start(bf16[256,1408]{1,0:T(8,128)(2,1)} %get-tuple-element.6) | copy-start | bytes 2162692
  114.6 2.0 %copy-start = (bf16[256,1408]{1,0:T(8,128)(2,1)S(1)}, bf16[256,1408]{1,0:T(8,128)(2,1)}, u32[]{:S(2)}) copy-start(bf16[256,1408]{1,0:T(8,128)(2,1)} %get-tuple-element.7) | copy-start | bytes 2162692

commit v5 on v4

--- a/solution.py
+++ b/solution.py
@@ -548,8 +548,8 @@
     early.finish()
     late.last(2)
     late.last(3)
+    late.spread(total)
     early.pass_on()
-    late.spread(total)
     gin[...] = (
         dot_t(dq[...], wv[0].reshape(D, HH))
         + dot_t(dk[...], wv[1].reshape(D, HH))

time: 118 us -> 117 us (level)
  no operation moved by 1% of the time
where the time goes in v5:
time: 117 us
  Pallas kernels  109 us (93%)
  local copies, waits for them, and re-layouts  7.04 us (6%)
    pallas_call x1, Pallas kernels, sublayer(): pl.pallas_call(sublayer_kernel, out_shape=(jax.ShapeDtypeStruct((OWN, D),...  109 us
    unnamed x9, local copies, waits for them, and re-layouts  5.85 us

profile of v5, /device:TPU:1, one launch (start us, length us, event | category | flops | bytes accessed | tf_op | source)
XLA Modules:
  0.0 117.0 jit_solution(9292857935338735215)
XLA Ops:
  0.6 1.7 %copy.14 = bf16[44,4,704]{2,0,1:T(8,128)(2,1)} copy(bf16[44,4,704]{2,1,0:T(4,128)(2,1)} %param.7) | data formatting | bytes 495616 | tf_op args[1]
  2.3 1.3 %copy.15 = s32[1,16,5]{1,2,0:T(8,128)} copy(s32[1,16,5]{1,0,2:T(1,128)} %param.9) | data formatting | bytes 640
  3.6 109.3 %sublayer.1 = (bf16[256,1408]{1,0:T(8,128)(2,1)}, bf16[256,1408]{1,0:T(8,128)(2,1)}, f32[4,88,704]{2,1,0:T(8,128)}) custom-call(bf16[4,44,704]{2,1,0:T(8,128)(2,1)} %bitcast.16, bf16[256,1408]{1,0:T(8,128)(2,1)} %bitcast.17, bf16[256,1408]{1,0:T(8,128)(2,1)} %bitcast.18, s32[5,16]{1,0:T(8,128)} %bitcast.21, s32[5]{0:T(128)} %bitcast.23, s32[16,128]{1,0:T(8,128)} %bitcast.22), custom_call_target="tpu_custom_call" | custom-call | tf_op jit(solution)/shard_map/sublayer/pallas_call | solution.py:602
  112.9 0.0 copy-start.1
  113.0 1.2 %dynamic-slice_bitcast_fusion = f32[44,4,704]{2,0,1:T(8,128)S(1)} fusion(f32[4,88,704]{2,1,0:T(8,128)} %get-tuple-element.8, s32[]{:T(128)S(6)} %select_n.11), kind=kLoop, calls=%fused_computation | loop fusion | bytes 991236 | tf_op jit(solution)/shard_map/transpose | solution.py:631
  114.2 0.0 copy-start
  114.2 1.1 copy.10
  115.3 0.0 copy-done.1
  115.3 0.9 copy.18
  116.2 0.0 copy-done
  116.2 0.9 copy.19
Async XLA Ops:
  112.9 2.4 %copy-start.1 = (bf16[256,1408]{1,0:T(8,128)(2,1)S(1)}, bf16[256,1408]{1,0:T(8,128)(2,1)}, u32[]{:S(2)}) copy-start(bf16[256,1408]{1,0:T(8,128)(2,1)} %get-tuple-element.6) | copy-start | bytes 2162692
  114.2 2.0 %copy-start = (bf16[256,1408]{1,0:T(8,128)(2,1)S(1)}, bf16[256,1408]{1,0:T(8,128)(2,1)}, u32[]{:S(2)}) copy-start(bf16[256,1408]{1,0:T(8,128)(2,1)} %get-tuple-element.7) | copy-start | bytes 2162692
